TPU v7x, 32 devices: a whole 2x2x4 slice. The times are simulated.
32 devices in a mesh: layer: 4 (over y, x), width: 8 (over z, core).
Axes of the slice: x: 2, y: 2, z: 4, core: 2. Of those that a mesh axis runs over, the one named last changes fastest.
Arguments:
- source: bfloat16 [4, 4096, 4096], P('layer', 'width'), may hold values from -6 to 6
- expand_out: bfloat16 [2560, 4096], P(None, 'width'), may hold values from -0.125 to 0.125
- expand_in: bfloat16 [2560, 4096], P(('layer', 'width')), may hold values from -0.09375 to 0.09375
- depth: float32 [8, 4], P('layer'), may hold values from -1.4 to 1.4
Outputs:
- grown: float32 [8, 2560, 2560], P('layer', 'width')
All inputs are finite; a program needn't handle non-finite values.
Results may differ from a plain program's by a relative error of at most 0.018.
Values may be sent and summed in bfloat16 or wider, within the bound.
No kernel may reach another device: no remote copies, remote signals or barrier semaphores. Data moves between devices by JAX's collectives and lax.ppermute only.
A program may use at most 128 MiB of HBM per device.

v0:
```python
import jax
import jax.numpy as jnp
from jax import lax
from jax.sharding import PartitionSpec as P


def on_device(source, expand_out, expand_in, depth):
    src_held, row_count, inner_width = source.shape
    stacked = source.reshape(src_held * row_count, inner_width)
    projected = lax.dot_general(
        stacked,
        lax.all_gather(expand_in, ("layer", "width"), axis=0, tiled=True),
        (((1,), (1,)), ((), ())),
        preferred_element_type=jnp.float32,
    )
    columns = projected.shape[1]
    projected = projected.astype(jnp.bfloat16).reshape(src_held, row_count, columns)
    own_rows = expand_out.shape[0] // lax.axis_size("width")
    partial_value = jnp.einsum(
        "ri,kic->rkc", expand_out, projected, preferred_element_type=jnp.float32
    ).astype(jnp.bfloat16)
    partial_value = lax.optimization_barrier(partial_value)
    summed = lax.psum_scatter(
        partial_value.astype(jnp.float32)
        .reshape(own_rows * lax.axis_size("width"), src_held * columns)
        .astype(jnp.bfloat16),
        "width",
        scatter_dimension=0,
        tiled=True,
    )
    expanded = summed.reshape(own_rows, src_held, columns)
    return jnp.einsum(
        "tm,rmc->trc",
        depth,
        lax.all_gather(expanded, "layer", axis=1, tiled=True).astype(jnp.float32),
        precision=lax.Precision.HIGHEST,
        preferred_element_type=jnp.float32,
    )


def solution(mesh):
    return jax.shard_map(
        on_device,
        mesh=mesh,
        in_specs=(
            P("layer", "width", None),
            P(None, "width"),
            P(("layer", "width"), None),
            P("layer", None),
        ),
        out_specs=P("layer", "width", None),
        check_vma=False,
    )
```

profile of v0, /device:TPU:0, one launch (start us, length us, event | category | flops | bytes accessed | tf_op | source)
XLA Modules:
  0.0 446.2 jit_solution(12219355690558130462)
XLA Ops:
  6.5 0.0 copy-start
  6.5 0.0 all-gather.4.cloned.1.call-start
  6.5 0.7 all-gather.4.cloned.1.call-update
  7.3 0.0 reduce-scatter.4.cloned.1.call-start
  7.3 139.5 %all-gather.4.cloned.1.call-done = bf16[2560,4096]{1,0:T(8,128)(2,1)} async-done(((bf16[80,4096]{1,0:T(8,128)(2,1)}), bf16[2560,4096]{1,0:T(8,128)(2,1)}) %all-gather.4.cloned.1.call-update) | async-done | bytes 20971536 | tf_op jit(solution)/shard_map/all_gather | solution.py:12
  146.8 0.0 copy-done
  146.8 26.9 %fusion = bf16[2560,1,2560]{0,2,1:T(8,128)(2,1)} fusion(bf16[2560,512]{1,0:T(8,128)(2,1)S(1)} %copy-done, bf16[2560,4096]{1,0:T(8,128)(2,1)} %all-gather.4.cloned.1.call-done, bf16[1,512,4096]{2,1,0:T(8,128)(2,1)} %param.4), kind=kOutput, calls=%fused_computation.1 | convolution fusion | flops 17456168960 | bytes 40894464 | tf_op jit(solution)/shard_map/ri,kic->rkc/dot_general | solution.py:19
  173.7 17.7 %copy.10 = bf16[2560,2560]{1,0:T(8,128)(2,1)} copy(bf16[2560,2560]{0,1:T(8,128)(2,1)} %bitcast.20) | data formatting | bytes 26214400
  191.4 0.0 reduce-scatter.4.cloned.1.call-update
  191.4 0.2 all-gather.6.cloned.1.call-start
  191.6 132.2 %reduce-scatter.4.cloned.1.call-done = bf16[320,2560]{1,0:T(8,128)(2,1)} async-done(((bf16[2560,2560]{1,0:T(8,128)(2,1)}), bf16[320,2560]{1,0:T(8,128)(2,1)}) %reduce-scatter.4.cloned.1.call-update) | async-done | bytes 1638416
  323.8 3.8 copy.11
  327.6 0.0 all-gather.6.cloned.1.call-update
  327.7 81.7 %all-gather.6.cloned.1.call-done = bf16[320,10240]{0,1:T(8,128)(2,1)} async-done(((bf16[320,2560]{0,1:T(8,128)(2,1)}), bf16[320,10240]{0,1:T(8,128)(2,1)}) %all-gather.6.cloned.1.call-update) | async-done | bytes 6553616 | tf_op jit(solution)/shard_map/all_gather | solution.py:35
  409.4 0.0 copy-start.2
  409.4 13.7 %copy.9 = bf16[320,4,2560]{2,1,0:T(4,128)(2,1)} copy(bf16[320,4,2560]{0,2,1:T(8,128)(2,1)} %bitcast.21) | data formatting | bytes 13107200 | tf_op jit(solution)/shard_map/all_gather | solution.py:35
  423.1 0.0 copy-done.2
  423.1 0.0 copy-start.1
  423.1 12.6 %convolution_bitcast_fusion = f32[2,320,2560]{2,0,1:T(2,128)S(1)} fusion(bf16[320,4,2560]{2,1,0:T(4,128)(2,1)} %copy.9, f32[2,4]{1,0:T(2,128)S(1)} %copy-done.2), kind=kOutput, calls=%fused_computation.2 | convolution fusion | flops 78643200 | bytes 13107232 | tf_op jit(solution)/shard_map/tm,rmc->trc/dot_general | solution.py:32
  435.7 4.0 copy.8
  439.7 0.0 copy-done.1
Async XLA Ops:
  6.5 140.2 %copy-start = (bf16[2560,512]{1,0:T(8,128)(2,1)S(1)}, bf16[2560,512]{1,0:T(8,128)(2,1)}, u32[]{:S(2)}) copy-start(bf16[2560,512]{1,0:T(8,128)(2,1)} %param.5) | copy-start | bytes 7864324
  6.5 140.2 %all-gather.4.cloned.1.call-start = ((), (), s32[]{:S(2)}) async-start(), calls=%async_computation.1 | async-start | bytes 21626880 | tf_op jit(solution)/shard_map/all_gather | solution.py:12
  7.3 316.6 %reduce-scatter.4.cloned.1.call-start = ((), (), s32[]{:S(2)}) async-start(), calls=%async_computation.3 | async-start | bytes 14745600
  191.4 218.0 %all-gather.6.cloned.1.call-start = ((), (), s32[]{:S(2)}) async-start(), calls=%async_computation.2 | async-start | bytes 9830400 | tf_op jit(solution)/shard_map/all_gather | solution.py:35
  409.4 13.7 %copy-start.2 = (f32[2,4]{1,0:T(2,128)S(1)}, f32[2,4]{1,0:T(2,128)}, u32[]{:S(2)}) copy-start(f32[2,4]{1,0:T(2,128)} %param.7) | copy-start | bytes 100
  423.1 16.6 %copy-start.1 = (bf16[2560,512]{1,0:T(8,128)(2,1)S(1)}, bf16[2560,512]{1,0:T(8,128)(2,1)}, u32[]{:S(2)}) copy-start(bf16[2560,512]{1,0:T(8,128)(2,1)} %param.5) | copy-start | bytes 7864324
Sparse Core Ops, SparseCore 0:
  10.2 136.5 all-gather.3
  191.5 132.2 reduce-scatter.3
  327.8 81.5 all-gather.5
where the time goes:
time: 447 us; the launch traced here: 446 us
  waiting for transfers between devices  354 us (79%)
  matrix products  39.5 us (9%)
  local copies, waits for them, and re-layouts  39.2 us (9%)
  between operations  13.1 us (3%)
    all_gather x1, waiting for transfers between devices, on_device(): lax.all_gather(expand_in, ('layer', 'width'), axis=0, tiled=True)  139 us
    unnamed x4, waiting for transfers between devices  133 us
    all_gather x1, waiting for transfers between devices, on_device(): lax.all_gather(expanded, 'layer', axis=1, tiled=True).astype(jnp.float32)  81.7 us
    dot_general x1, matrix products, on_device(): jnp.einsum('ri,kic->rkc', expand_out, projected, preferred_element_type=j...  26.9 us
    unnamed x8, local copies, waits for them, and re-layouts  21.5 us
    all_gather x1, local copies, waits for them, and re-layouts, on_device(): lax.all_gather(expanded, 'layer', axis=1, tiled=True).astype(jnp.float32)  13.7 us
    dot_general x1, matrix products, on_device(): jnp.einsum('tm,rmc->trc', depth, lax.all_gather(expanded, 'layer', axis=1...  12.6 us
  transfers between devices with their start and end apart: 3, of which 3 were waited for; matrix products, arithmetic and copies ran while one was open for 0% of the time, Pallas kernels for 0%

commit v1 on v0

v1 whole, which is shorter than its diff:
```python
import jax
import jax.numpy as jnp
from jax import lax
from jax.experimental import pallas as pl
from jax.experimental.pallas import tpu as pltpu
from jax.sharding import PartitionSpec as P

AXES = ("layer", "width")
GROUPS = (1, 2, 2)
LANES = 128
PACK = 16


def splits(total, parts):
    edges = [total * p // parts for p in range(parts + 1)]
    return list(zip(edges[:-1], edges[1:]))


class Moves:
    def __init__(self, layers, chips, cores):
        self.layers, self.chips, self.cores = layers, chips, cores

    def send(self, value, target, senders=None):
        pairs = []
        for k in range(self.layers):
            for z in range(self.chips):
                for c in range(self.cores):
                    if senders is not None and z not in senders:
                        continue
                    pairs.append((self.at(k, z, c), self.at(*target(k, z, c))))
        return lax.ppermute(value, AXES, pairs)

    def at(self, k, z, c):
        return (k * self.chips + z) * self.cores + c

    def partner(self, value):
        return self.send(value, lambda k, z, c: (k, z, self.cores - 1 - c))

    def across(self, value, bit):
        return self.send(value, lambda k, z, c: (k ^ (1 << bit), z, c))

    def up(self, value, senders):
        return self.send(value, lambda k, z, c: (k, z + 1, c), senders)

    def down(self, value, senders):
        return self.send(value, lambda k, z, c: (k, z - 1, c), senders)


def line_gather(moves, own, z):
    n = moves.chips
    low, high = [own], [own]
    for hop in range(1, n):
        low.append(moves.up(low[-1], range(hop - 1, n - 1)))
        high.append(moves.down(high[-1], range(1, n - hop + 1)))
    blocks = []
    for b in range(n):
        held = own
        for at in range(n):
            if at > b:
                held = jnp.where(z == at, low[at - b], held)
            elif at < b:
                held = jnp.where(z == at, high[b - at], held)
        blocks.append(held)
    return jnp.concatenate(blocks, axis=0)


def cube_gather(moves, own):
    bits = moves.layers.bit_length() - 1
    held = {0: own}
    for weight in range(1, bits + 1):
        fresh = {}
        for rel in range(1, moves.layers):
            ways = [b for b in range(bits) if rel >> b & 1]
            if len(ways) != weight:
                continue
            parts = []
            for bit, (lo, hi) in zip(reversed(ways), splits(own.shape[0], weight)):
                parts.append(moves.across(held[rel ^ (1 << bit)][lo:hi], bit))
            fresh[rel] = parts[0] if weight == 1 else jnp.concatenate(parts, axis=0)
        held.update(fresh)
    return [held[rel] for rel in range(moves.layers)]


def line_scatter(moves, terms, z):
    n = moves.chips
    pick = lambda b: lax.dynamic_index_in_dim(terms, jnp.clip(b, 0, n - 1), 0, keepdims=False)
    add = lambda a, b: (a.astype(jnp.float32) + b.astype(jnp.float32)).astype(jnp.bfloat16)
    from_low = from_high = None
    for hop in range(1, n):
        low, high = pick(n + z - hop), pick(z + hop - n)
        if hop > 1:
            low, high = add(low, from_low), add(high, from_high)
        from_low = moves.up(low, range(0, hop))
        from_high = moves.down(high, range(n - hop, n))
    own = pick(z).astype(jnp.float32)
    return (own + from_low.astype(jnp.float32) + from_high.astype(jnp.float32)).astype(jnp.bfloat16)


def mm(a, b):
    return lax.dot_general(a, b, (((1,), (1,)), ((), ())), preferred_element_type=jnp.float32)


def spread_plan(source, expand_out, expand_in, depth):
    cores = 2
    layers, width = lax.axis_size("layer"), lax.axis_size("width")
    chips = width // cores
    moves = Moves(layers, chips, cores)
    me, w = lax.axis_index("layer"), lax.axis_index("width")
    z, core = w // cores, w % cores
    rows = expand_out.shape[0]
    own_rows = rows // width
    chip_rows = rows // chips
    mine = source.reshape(source.shape[0] * source.shape[1], source.shape[2])
    theirs = moves.partner(mine)
    out_mine = expand_out
    out_theirs = moves.partner(expand_out)
    held = expand_in.shape[0]
    window = -(-own_rows // LANES) * LANES
    if window > chip_rows:
        window = own_rows
    first = chip_rows - window

    if held % (PACK * sum(GROUPS)) == 0:
        unit = held // sum(GROUPS)
        edges = [0]
        for g in GROUPS:
            edges.append(edges[-1] + g * unit)
    else:
        edges = [0, held]

    pieces = []
    for lo, hi in zip(edges[:-1], edges[1:]):
        block = line_gather(moves, expand_in[lo:hi], z)
        chunk = jnp.concatenate(cube_gather(moves, block), axis=0)
        left = mm(chunk, mine).astype(jnp.bfloat16)
        right = mm(chunk, theirs).astype(jnp.bfloat16)
        terms = (mm(left, out_mine) + mm(right, out_theirs)).astype(jnp.bfloat16)
        terms = terms.reshape(terms.shape[0], chips, chip_rows).transpose(1, 0, 2)
        expanded = line_scatter(moves, terms, z)
        spread = jnp.stack(cube_gather(moves, expanded))
        keep = jnp.where(core == 0, spread[..., :window], spread[..., first:])
        give = jnp.where(core == 0, spread[..., first:], spread[..., :window])
        pieces.append((keep, moves.partner(give), hi - lo))

    by_core = []
    for which in range(cores):
        parts = [
            jnp.where(core == which, keep, got).reshape(layers, layers, chips, h, window)
            for keep, got, h in pieces
        ]
        by_core.append(jnp.concatenate(parts, axis=3))
    full = jnp.stack(by_core, axis=3)
    offset = jnp.where(core == 0, 0, own_rows - first)
    full = lax.dynamic_slice_in_dim(full, offset, own_rows, 5).astype(jnp.float32)
    grown = []
    index = jnp.arange(layers)
    for target in range(layers):
        col = full[index, index ^ me ^ target]
        weight = depth[:, index ^ me]
        grown.append(jnp.einsum("td,dznhr->trznh", weight, col, precision=lax.Precision.HIGHEST).reshape(depth.shape[0], own_rows, -1))
    return jnp.concatenate(grown, axis=2)


NT = (((1,), (1,)), ((), ()))

PIECES = (((0, 0),), ((0, 1), (1, 0)), ((2, 0), (1, 1)), ((2, 1), (3, 0)), ((3, 1),))


def project(units, h, inner, mine, theirs):
    depth = mine.shape[1]
    n = len(units)
    flat = [x for unit in units for x in unit]
    held = mine.shape[0]
    tile = min(256, held)
    steps = held // tile
    c = 2 * n * h

    def kernel(inner_ref, *refs):
        e, (own_ref, far_ref, out_ref, lhs) = refs[: 3 * n], refs[3 * n :]
        step = pl.program_id(0)

        @pl.when(step == 0)
        def _():
            for u in range(n):
                a, b, third = e[3 * u : 3 * u + 3]

                low = pl.ds(pl.multiple_of(2 * u * h + inner_ref[1] * h, PACK), h)
                high = pl.ds(pl.multiple_of((2 * u + 1) * h - inner_ref[1] * h, PACK), h)

                if a is b:
                    lhs[low, :] = a[...]
                else:

                    @pl.when(inner_ref[0] == 1)
                    def _():
                        lhs[low, :] = a[...]

                    @pl.when(inner_ref[0] == 0)
                    def _():
                        lhs[low, :] = b[...]

                lhs[high, :] = third[...]

        @pl.when(step < steps)
        def _():
            out_ref[...] = lax.dot_general(lhs[...], own_ref[...], NT, preferred_element_type=jnp.float32).astype(jnp.bfloat16)

        @pl.when(step >= steps)
        def _():
            out_ref[...] = lax.dot_general(lhs[...], far_ref[...], NT, preferred_element_type=jnp.float32).astype(jnp.bfloat16)

    return pl.pallas_call(
        kernel,
        grid_spec=pltpu.PrefetchScalarGridSpec(
            num_scalar_prefetch=1,
            grid=(2 * steps,),
            in_specs=[pl.BlockSpec((h, depth), lambda i, s: (0, 0), pipeline_mode=pl.Buffered(1))] * len(flat)
            + [
                pl.BlockSpec((tile, depth), lambda i, s: (jnp.minimum(i, steps - 1), 0)),
                pl.BlockSpec((tile, depth), lambda i, s: (jnp.maximum(i - steps, 0), 0)),
            ],
            out_specs=pl.BlockSpec((c, tile), lambda i, s: (0, i)),
            scratch_shapes=[pltpu.VMEM((c, depth), jnp.bfloat16)],
        ),
        out_shape=jax.ShapeDtypeStruct((c, 2 * held), jnp.bfloat16),
        compiler_params=pltpu.CompilerParams(vmem_limit_bytes=22 << 20, dimension_semantics=("arbitrary",)),
        cost_estimate=pl.CostEstimate(
            flops=4 * c * depth * held,
            bytes_accessed=2 * (c * depth + 2 * held * depth + 2 * c * held),
            transcendentals=0,
        ),
        name="project",
    )(inner, *flat, mine, theirs)


def expand(order, near, outs, chip_rows):
    c, depth = near.shape
    half = depth // 2
    steps = 4

    def kernel(order_ref, near_ref, own_ref, far_ref, give_ref, keep_ref):
        got = lax.dot_general(near_ref[:, :half], own_ref[...], NT, preferred_element_type=jnp.float32)
        got += lax.dot_general(near_ref[:, half:], far_ref[...], NT, preferred_element_type=jnp.float32)
        got = got.astype(jnp.bfloat16)
        step = pl.program_id(0)

        @pl.when(step < 2)
        def _():
            give_ref[0] = got

        @pl.when(step >= 2)
        def _():
            keep_ref[0] = got

    return pl.pallas_call(
        kernel,
        grid_spec=pltpu.PrefetchScalarGridSpec(
            num_scalar_prefetch=1,
            grid=(steps,),
            in_specs=[
                pl.BlockSpec((c, depth), lambda i, o: (0, 0)),
                pl.BlockSpec((chip_rows, half), lambda i, o: (o[i], 0)),
                pl.BlockSpec((chip_rows, half), lambda i, o: (o[i], 0)),
            ],
            out_specs=[
                pl.BlockSpec((1, c, chip_rows), lambda i, o: (jnp.minimum(i, 1), 0, 0)),
                pl.BlockSpec((1, c, chip_rows), lambda i, o: (jnp.maximum(i - 2, 0), 0, 0)),
            ],
        ),
        out_shape=[jax.ShapeDtypeStruct((2, c, chip_rows), jnp.bfloat16)] * 2,
        compiler_params=pltpu.CompilerParams(vmem_limit_bytes=12 << 20, dimension_semantics=("arbitrary",)),
        cost_estimate=pl.CostEstimate(
            flops=2 * c * depth * chip_rows * steps,
            bytes_accessed=2 * (c * depth + steps * (chip_rows * depth + c * chip_rows)),
            transcendentals=0,
        ),
        name="expand",
    )(order, near, *outs)


def hand_over(start, parts, counts, window):
    width = window // LANES
    c = parts[0].shape[0]
    sources = sum(counts) // c

    def kernel(start_ref, *refs):
        out_ref = refs[-1]
        row = 0
        for ref in refs[:-1]:
            n = ref.shape[0]
            out_ref[row // c, row % c : row % c + n, :] = ref[...]
            row += n

    return pl.pallas_call(
        kernel,
        grid_spec=pltpu.PrefetchScalarGridSpec(
            num_scalar_prefetch=1,
            grid=(width,),
            in_specs=[pl.BlockSpec((n, LANES), lambda i, s: (0, s[0] + i)) for n in counts],
            out_specs=pl.BlockSpec((sources, c, LANES), lambda i, s: (0, 0, i)),
        ),
        out_shape=jax.ShapeDtypeStruct((sources, c, window), parts[0].dtype),
        compiler_params=pltpu.CompilerParams(vmem_limit_bytes=8 << 20, dimension_semantics=("arbitrary",)),
        cost_estimate=pl.CostEstimate(flops=0, bytes_accessed=4 * sources * c * window, transcendentals=0),
        name="hand_over",
    )(start, *parts)


def mix(info, weight, kept, given, own_rows, window, first, held, columns):
    sources = given[0].shape[0]
    rels = sources
    counts = [[part.shape[0] for part in row] for row in kept]
    flat_parts = [part for row in kept for part in row]
    unit = 2 * held
    slots = 4
    targets = weight.shape[0]
    tall = 2 * slots * held
    pieces = len(PIECES)

    def kernel(info_ref, w_ref, *refs):
        total = len(flat_parts)
        flat = refs[:total]
        got = refs[total : total + pieces]
        out_ref, own, other, acc, turned, sems = refs[total + pieces :]
        step = pl.program_id(0)
        me, core = info_ref[0], info_ref[1]
        lane = pl.multiple_of(core * first, LANES)

        def copies(ring):
            for p, units in enumerate(PIECES):
                for u, (rel, kind) in enumerate(units):
                    for d in range(sources):
                        if rel ^ d != ring:
                            continue
                        yield pltpu.make_async_copy(
                            got[p].at[d, pl.ds(u * unit, unit)],
                            other.at[rel, d, pl.ds(kind * unit, unit)],
                            sems.at[ring],
                        )
                        want = d * len(units) * unit + u * unit
                        row = 0
                        for k, n in enumerate(counts[p]):
                            lo, hi = max(want, row), min(want + unit, row + n)
                            if lo < hi:
                                yield pltpu.make_async_copy(
                                    flat[sum(map(len, counts[:p])) + k].at[pl.ds(lo - row, hi - lo), pl.ds(lane, window)],
                                    own.at[rel, d, pl.ds(kind * unit + lo - want, hi - lo)],
                                    sems.at[ring],
                                )
                            row += n

        @pl.when(step == 0)
        def _():
            for ring in range(rels):
                for copy in copies(ring):
                    copy.start()

        for ring in range(rels):

            @pl.when(step == ring)
            def _():
                for copy in copies(ring):
                    copy.wait()

        for s in range(slots):
            z = info_ref[2 + s]
            for which in range(2):
                held_at = own if which == 0 else other
                base = z * unit + (core if which == 0 else 1 - core) * held
                base = pl.multiple_of(base, PACK)
                sums = [None] * targets
                for d in range(sources):
                    rel = step ^ d
                    value = held_at[rel, d, s * held : (s + 1) * held, :].astype(jnp.float32)
                    for t in range(targets):
                        term = value * w_ref[t, me ^ d]
                        sums[t] = term if d == 0 else sums[t] + term
                for t in range(targets):
                    acc[t, pl.ds(base, held), :] = sums[t]
        shift = pl.multiple_of(core * (own_rows - first), PACK)
        for t in range(targets):
            turned[...] = acc[t].T
            out_ref[t] = turned[pl.ds(shift, own_rows), :]

    return pl.pallas_call(
        kernel,
        grid_spec=pltpu.PrefetchScalarGridSpec(
            num_scalar_prefetch=2,
            grid=(rels,),
            in_specs=[pl.BlockSpec(memory_space=pl.ANY)] * (len(flat_parts) + pieces),
            out_specs=pl.BlockSpec((targets, own_rows, tall), lambda i, a, b: (0, 0, i ^ a[0])),
            scratch_shapes=[
                pltpu.VMEM((rels, sources, slots * held, window), jnp.bfloat16),
                pltpu.VMEM((rels, sources, slots * held, window), jnp.bfloat16),
                pltpu.VMEM((targets, tall, window), jnp.float32),
                pltpu.VMEM((window, tall), jnp.float32),
                pltpu.SemaphoreType.DMA((rels,)),
            ],
        ),
        out_shape=jax.ShapeDtypeStruct((targets, own_rows, columns), jnp.float32),
        compiler_params=pltpu.CompilerParams(dimension_semantics=("arbitrary",)),
        name="mix",
    )(info, weight, *flat_parts, *given)


def fold_plan(source, expand_out, expand_in, depth):
    cores = 2
    layers, width = lax.axis_size("layer"), lax.axis_size("width")
    chips = width // cores
    moves = Moves(layers, chips, cores)
    me, w = lax.axis_index("layer"), lax.axis_index("width")
    z, core = w // cores, w % cores
    rows, columns = expand_out.shape[0], expand_in.shape[0] * layers * width
    own_rows, chip_rows = rows // width, rows // chips
    window = -(-own_rows // LANES) * LANES
    first = chip_rows - window
    h = expand_in.shape[0]
    right = z >= chips // 2
    inner = jnp.logical_and(z > 0, z < chips - 1)

    pair = lambda v: moves.send(v, lambda k, z, c: (k, z ^ 1, c))
    middle = lambda v: moves.send(v, lambda k, z, c: (k, 3 - z if z in (1, 2) else z, c))
    mirror = lambda v: moves.send(v, lambda k, z, c: (k, 3 - z, c))
    over_x = lambda v: moves.across(v, 0)
    over_y = lambda v: moves.across(v, 1)
    partner = moves.partner

    mine = source.reshape(source.shape[0] * source.shape[1], source.shape[2])
    own = expand_in
    near_z = pair(own)
    mid_a = middle(own)
    x0, y0 = over_x(own), over_y(own)
    theirs = partner(mine)
    outs = (expand_out, partner(expand_out))
    mid_b = middle(near_z)
    out_b = pair(mid_a)
    x1, y1 = over_x(near_z), over_y(near_z)
    choose = lambda a, b: jnp.where(inner, a, b)
    third = choose(mid_a, out_b)
    out_c = pair(mid_b)
    x2, y2 = over_x(third), over_y(third)
    fourth = choose(mid_b, out_c)
    x3, y3 = over_x(fourth), over_y(fourth)
    d0, d2 = over_x(jnp.where(inner, y0, y1)), over_y(x2)
    d1, d3 = over_x(jnp.where(inner, y1, y0)), over_y(x3)
    held = [(own, near_z, third, fourth), (x0, x1, x2, x3), (y0, y1, y2, y3)]

    def unit(rel, kind):
        if rel == 3:
            return (d0, d0, d2) if kind == 0 else (d1, d1, d3)
        a, b, c, d = held[rel]
        return (a, b, c) if kind == 0 else (b, a, d)

    flip = lambda m: jnp.where(right, chips - 1 - m, m)
    ints = lambda *v: jnp.stack([jnp.asarray(x, jnp.int32) for x in v])
    order = ints(*[flip(jnp.where(inner, m, e)) for m, e in ((0, 1), (3, 2), (1, 0), (2, 3))])
    place = ints(inner, right)
    f32 = jnp.float32

    kept, given = [], []
    for piece in PIECES:
        near = project([unit(*u) for u in piece], h, place, mine, theirs)
        give, keep = expand(order, near, outs, chip_rows)
        got = pair(give)
        last = mirror((keep[1].astype(f32) + got[1].astype(f32)).astype(jnp.bfloat16))
        expanded = (keep[0].astype(f32) + got[0].astype(f32) + last.astype(f32)).astype(jnp.bfloat16)
        from_x, from_y = over_x(expanded), over_y(expanded)
        cut = expanded.shape[0] // 2
        low, high = over_x(from_y[:cut]), over_y(from_x[cut:])
        spread = [expanded, from_x, from_y, low, high]
        start = ints(jnp.where(core == 0, first // LANES, 0))
        give = hand_over(start, spread, [part.shape[0] for part in spread], window)
        kept.append(spread)
        given.append(partner(give))

    info = ints(me, core, 1, 2, 0, 3)
    return mix(info, depth, kept, given, own_rows, window, first, h, columns)


def on_device(source, expand_out, expand_in, depth):
    chips = lax.axis_size("width") // 2
    aligned = expand_in.shape[0] % PACK == 0 and expand_out.shape[0] % (chips * LANES) == 0
    plan = fold_plan if chips == 4 and lax.axis_size("layer") == 4 and aligned else spread_plan
    return plan(source, expand_out, expand_in, depth)


def solution(mesh):
    return jax.shard_map(
        on_device,
        mesh=mesh,
        in_specs=(
            P("layer", "width", None),
            P(None, "width"),
            P(("layer", "width"), None),
            P("layer", None),
        ),
        out_specs=P("layer", "width", None),
        check_vma=False,
    )
```

time: 447 us -> 265 us (0.59)
  waiting for transfers between devices: 354 us -> 115 us
  starting transfers between devices: 0.26 us -> 79.8 us
  Pallas kernels: 0 us -> 64.6 us
  matrix products: 39.5 us -> 0 us
  local copies, waits for them, and re-layouts: 39.2 us -> 1.89 us
  between operations: 13.1 us -> 0.76 us
    all_gather x2 -> x0, waiting for transfers between devices: 221 us -> none  [the longest x1 139 us: on_device(): lax.all_gather(expand_in, ('layer', 'width'), axis=0, tiled=True)]
    unnamed x4 -> x0, waiting for transfers between devices: 133 us -> none
    ppermute x0 -> x54, waiting for transfers between devices: none -> 115 us  [send(): return lax.ppermute(value, AXES, pairs)]
    ppermute x0 -> x54, starting transfers between devices: none -> 79.8 us  [send(): return lax.ppermute(value, AXES, pairs)]
    pallas_call x0 -> x16, Pallas kernels: none -> 64.6 us  [the longest x5 32.8 us: project(): pl.pallas_call(kernel, grid_spec=pltpu.PrefetchScalarGridSpec(num_scalar_...]
    dot_general x2 -> x0, matrix products: 39.5 us -> none  [the longest x1 26.9 us: on_device(): jnp.einsum('ri,kic->rkc', expand_out, projected, preferred_element_type=j...]
    unnamed x8 -> x58, local copies, waits for them, and re-layouts: 21.5 us -> 1.08 us
    all_gather x1 -> x0, local copies, waits for them, and re-layouts: 13.7 us -> none  [on_device(): lax.all_gather(expanded, 'layer', axis=1, tiled=True).astype(jnp.float32)]
  transfers between devices with their start and end apart: 3 -> 54, of which waited for: 3 -> 21; matrix products, arithmetic and copies ran while one was open for 0% -> 1% of each run, Pallas kernels for 0% -> 21%
where the time goes in v1:
time: 265 us; the launch traced here: 264 us
  waiting for transfers between devices  115 us (43%)
  starting transfers between devices  79.8 us (30%)
  Pallas kernels  64.6 us (24%)
    ppermute x54, waiting for transfers between devices, send(): return lax.ppermute(value, AXES, pairs)  115 us
    ppermute x54, starting transfers between devices, send(): return lax.ppermute(value, AXES, pairs)  79.8 us
    pallas_call x5, Pallas kernels, project(): pl.pallas_call(kernel, grid_spec=pltpu.PrefetchScalarGridSpec(num_scalar_...  32.8 us
    pallas_call x5, Pallas kernels, expand(): pl.pallas_call(kernel, grid_spec=pltpu.PrefetchScalarGridSpec(num_scalar_...  16.6 us
    pallas_call x1, Pallas kernels, mix(): pl.pallas_call(kernel, grid_spec=pltpu.PrefetchScalarGridSpec(num_scalar_...  9.14 us
    pallas_call x5, Pallas kernels, hand_over(): pl.pallas_call(kernel, grid_spec=pltpu.PrefetchScalarGridSpec(num_scalar_...  6.1 us
  transfers between devices with their start and end apart: 54, of which 21 were waited for; matrix products, arithmetic and copies ran while one was open for 1% of the time, Pallas kernels for 21%

profile of v1, /device:TPU:0, one launch (start us, length us, event | category | flops | bytes accessed | tf_op | source)
XLA Modules:
  0.0 264.1 jit_solution(13638633983609615529)
XLA Ops:
  2.2 4.5 %collective-permute-start = (bf16[80,4096]{1,0:T(8,128)(2,1)}, bf16[80,4096]{1,0:T(8,128)(2,1)S(1)}, u32[]{:S(2)}, u32[]{:S(2)}) collective-permute-start(bf16[80,4096]{1,0:T(8,128)(2,1)} %refs_1_.1), channel_id=1, source_target_pairs={{0,2},{1,3},{2,0},{3,1},{4,6},{5,7},{6,4},{7,5},{8,10},{9,11},{10,... | collective-permute-start | bytes 1966088 | tf_op jit(solution)/shard_map/ppermute | solution.py:31
  6.7 15.5 %collective-permute-start.2 = (bf16[80,4096]{1,0:T(8,128)(2,1)S(1)}, bf16[80,4096]{1,0:T(8,128)(2,1)}, u32[]{:S(2)}, u32[]{:S(2)}) collective-permute-start(bf16[80,4096]{1,0:T(8,128)(2,1)S(1)} %collective-permute-done.1), channel_id=1, source_target_pairs={{0,2},{1,3},{2,0},{3,1},{4,6},{5,7},{6,4},{7,5},{8,10},{9,11},{10,... | collective-permute-start | bytes 1966088 | tf_op jit(solution)/shard_map/ppermute | solution.py:31
  27.0 9.8 %collective-permute-done.2 = bf16[80,4096]{1,0:T(8,128)(2,1)} collective-permute-done((bf16[80,4096]{1,0:T(8,128)(2,1)S(1)}, bf16[80,4096]{1,0:T(8,128)(2,1)}, u32[]{:S(2)}, u32[]{:S(2)}) %collective-permute-start.2) | collective-permute-done | bytes 655392 | tf_op jit(solution)/shard_map/ppermute | solution.py:31
  36.8 4.7 %collective-permute-start.12 = (bf16[80,4096]{1,0:T(8,128)(2,1)}, bf16[80,4096]{1,0:T(8,128)(2,1)S(1)}, u32[]{:S(2)}, u32[]{:S(2)}) collective-permute-start(bf16[80,4096]{1,0:T(8,128)(2,1)} %collective-permute-done.11), channel_id=1, source_target_pairs={{0,2},{1,3},{2,0},{3,1},{4,6},{5,7},{6,4},{7,5},{8,10},{9,11},{10,... | collective-permute-start | bytes 1966088 | tf_op jit(solution)/shard_map/ppermute | solution.py:31
  44.3 10.8 %collective-permute-done.12 = bf16[80,4096]{1,0:T(8,128)(2,1)S(1)} collective-permute-done((bf16[80,4096]{1,0:T(8,128)(2,1)}, bf16[80,4096]{1,0:T(8,128)(2,1)S(1)}, u32[]{:S(2)}, u32[]{:S(2)}) %collective-permute-start.12) | collective-permute-done | bytes 655392 | tf_op jit(solution)/shard_map/ppermute | solution.py:31
  58.2 2.5 collective-permute-start.24
  60.7 11.9 %collective-permute-done.23.refs_1_.refs_0_ = bf16[80,4096]{1,0:T(8,128)(2,1)S(1)} collective-permute-done((bf16[80,4096]{1,0:T(8,128)(2,1)S(1)}, bf16[80,4096]{1,0:T(8,128)(2,1)S(1)}, u32[]{:S(2)}, u32[]{:S(2)}) %collective-permute-start.23) | collective-permute-done | bytes 655392 | tf_op jit(solution)/shard_map/ppermute | solution.py:31
  77.6 6.6 %project.6.near_ref = bf16[320,1024]{1,0:T(8,128)(2,1)S(1)} custom-call(s32[2]{0:T(128)S(1)} %add_convert_fusion.5.inner_ref, bf16[80,4096]{1,0:T(8,128)(2,1)S(1)} %collective-permute-done.refs_1_.refs_0_, bf16[80,4096]{1,0:T(8,128)(2,1)S(1)} %copy-done.5, bf16[80,4096]{1,0:T(8,128)(2,1)S(1)} %broadcast_select_fusion.2.refs_2_, ...), custom_call_target="tpu_custom_call" | custom-call | flops 2684354560 | bytes 11665408 | tf_op jit(solution)/shard_map/project/pallas_call | solution.py:212
  84.3 3.6 %expand.6 = (bf16[2,320,640]{2,1,0:T(8,128)(2,1)S(1)}, bf16[2,320,640]{2,1,0:T(8,128)(2,1)S(1)}) custom-call(s32[4]{0:T(128)S(1)} %pad_add_fusion.order_ref, bf16[320,1024]{1,0:T(8,128)(2,1)S(1)} %project.6.near_ref, bf16[2560,512]{1,0:T(8,128)(2,1)S(1)} %copy-done.1, bf16[2560,512]{1,0:T(8,128)(2,1)S(1)} %collective-permute-done.4.far_ref), custom_call_target="tpu_custom_call" | custom-call | flops 1677721600 | bytes 7536640 | tf_op jit(solution)/shard_map/expand/pallas_call | solution.py:255
  91.7 6.6 %project.7.near_ref = bf16[320,1024]{1,0:T(8,128)(2,1)S(1)} custom-call(s32[2]{0:T(128)S(1)} %add_convert_fusion.5.inner_ref, bf16[80,4096]{1,0:T(8,128)(2,1)S(1)} %collective-permute-done.22.refs_0_.refs_1_, bf16[80,4096]{1,0:T(8,128)(2,1)S(1)} %collective-permute-done.23.refs_1_.refs_0_, bf16[80,4096]{1,0:T(8,128)(2,1)S(1)} %collective-permute-done.24.refs_2_, ...), custom_call_target="tpu_custom_call" | custom-call | flops 2684354560 | bytes 11665408 | tf_op jit(solution)/shard_map/project/pallas_call | solution.py:212
  98.4 5.9 %collective-permute-done.33.refs_3_.refs_4_ = bf16[80,4096]{1,0:T(8,128)(2,1)S(1)} collective-permute-done((bf16[80,4096]{1,0:T(8,128)(2,1)S(1)}, bf16[80,4096]{1,0:T(8,128)(2,1)S(1)}, u32[]{:S(2)}, u32[]{:S(2)}) %collective-permute-start.33) | collective-permute-done | bytes 655392 | tf_op jit(solution)/shard_map/ppermute | solution.py:31
  106.0 3.6 %expand.7 = (bf16[2,320,640]{2,1,0:T(8,128)(2,1)S(1)}, bf16[2,320,640]{2,1,0:T(8,128)(2,1)S(1)}) custom-call(s32[4]{0:T(128)S(1)} %pad_add_fusion.order_ref, bf16[320,1024]{1,0:T(8,128)(2,1)S(1)} %project.7.near_ref, bf16[2560,512]{1,0:T(8,128)(2,1)S(1)} %copy-done.1, bf16[2560,512]{1,0:T(8,128)(2,1)S(1)} %collective-permute-done.4.far_ref), custom_call_target="tpu_custom_call" | custom-call | flops 1677721600 | bytes 7536640 | tf_op jit(solution)/shard_map/expand/pallas_call | solution.py:255
  109.9 4.8 %collective-permute-done.34.refs_5_ = bf16[80,4096]{1,0:T(8,128)(2,1)S(1)} collective-permute-done((bf16[80,4096]{1,0:T(8,128)(2,1)S(1)}, bf16[80,4096]{1,0:T(8,128)(2,1)S(1)}, u32[]{:S(2)}, u32[]{:S(2)}) %collective-permute-start.34) | collective-permute-done | bytes 655392 | tf_op jit(solution)/shard_map/ppermute | solution.py:31
  114.8 6.6 %project.8.near_ref = bf16[320,1024]{1,0:T(8,128)(2,1)S(1)} custom-call(s32[2]{0:T(128)S(1)} %add_convert_fusion.5.inner_ref, bf16[80,4096]{1,0:T(8,128)(2,1)S(1)} %collective-permute-done.23.refs_1_.refs_0_, bf16[80,4096]{1,0:T(8,128)(2,1)S(1)} %collective-permute-done.22.refs_0_.refs_1_, bf16[80,4096]{1,0:T(8,128)(2,1)S(1)} %collective-permute-done.32.refs_2_, ...), custom_call_target="tpu_custom_call" | custom-call | flops 2684354560 | bytes 11665408 | tf_op jit(solution)/shard_map/project/pallas_call | solution.py:212
  121.4 3.6 %expand.8 = (bf16[2,320,640]{2,1,0:T(8,128)(2,1)S(1)}, bf16[2,320,640]{2,1,0:T(8,128)(2,1)S(1)}) custom-call(s32[4]{0:T(128)S(1)} %pad_add_fusion.order_ref, bf16[320,1024]{1,0:T(8,128)(2,1)S(1)} %project.8.near_ref, bf16[2560,512]{1,0:T(8,128)(2,1)S(1)} %copy-done.1, bf16[2560,512]{1,0:T(8,128)(2,1)S(1)} %collective-permute-done.4.far_ref), custom_call_target="tpu_custom_call" | custom-call | flops 1677721600 | bytes 7536640 | tf_op jit(solution)/shard_map/expand/pallas_call | solution.py:255
  126.8 6.4 %project.5.near_ref = bf16[160,1024]{1,0:T(8,128)(2,1)S(1)} custom-call(s32[2]{0:T(128)S(1)} %add_convert_fusion.5.inner_ref, bf16[80,4096]{1,0:T(8,128)(2,1)S(1)} %copy-done.5, bf16[80,4096]{1,0:T(8,128)(2,1)S(1)} %collective-permute-done.refs_1_.refs_0_, bf16[80,4096]{1,0:T(8,128)(2,1)S(1)} %broadcast_select_fusion.3.refs_2_, ...), custom_call_target="tpu_custom_call" | custom-call | flops 1342177280 | bytes 10027008 | tf_op jit(solution)/shard_map/project/pallas_call | solution.py:212
  133.2 2.9 %expand.5 = (bf16[2,160,640]{2,1,0:T(8,128)(2,1)S(1)}, bf16[2,160,640]{2,1,0:T(8,128)(2,1)S(1)}) custom-call(s32[4]{0:T(128)S(1)} %pad_add_fusion.order_ref, bf16[160,1024]{1,0:T(8,128)(2,1)S(1)} %project.5.near_ref, bf16[2560,512]{1,0:T(8,128)(2,1)S(1)} %copy-done.1, bf16[2560,512]{1,0:T(8,128)(2,1)S(1)} %collective-permute-done.4.far_ref), custom_call_target="tpu_custom_call" | custom-call | flops 838860800 | bytes 6389760 | tf_op jit(solution)/shard_map/expand/pallas_call | solution.py:255
  136.4 6.4 %project.9.near_ref = bf16[160,1024]{1,0:T(8,128)(2,1)S(1)} custom-call(s32[2]{0:T(128)S(1)} %add_convert_fusion.5.inner_ref, bf16[80,4096]{1,0:T(8,128)(2,1)S(1)} %collective-permute-done.41.refs_0_.refs_1_, bf16[80,4096]{1,0:T(8,128)(2,1)S(1)} %collective-permute-done.41.refs_0_.refs_1_, bf16[80,4096]{1,0:T(8,128)(2,1)S(1)} %collective-permute-done.42.refs_2_, ...), custom_call_target="tpu_custom_call" | custom-call | flops 1342177280 | bytes 10027008 | tf_op jit(solution)/shard_map/project/pallas_call | solution.py:212
  142.9 3.0 %expand.9 = (bf16[2,160,640]{2,1,0:T(8,128)(2,1)S(1)}, bf16[2,160,640]{2,1,0:T(8,128)(2,1)S(1)}) custom-call(s32[4]{0:T(128)S(1)} %pad_add_fusion.order_ref, bf16[160,1024]{1,0:T(8,128)(2,1)S(1)} %project.9.near_ref, bf16[2560,512]{1,0:T(8,128)(2,1)S(1)} %copy-done.1, bf16[2560,512]{1,0:T(8,128)(2,1)S(1)} %collective-permute-done.4.far_ref), custom_call_target="tpu_custom_call" | custom-call | flops 838860800 | bytes 6389760 | tf_op jit(solution)/shard_map/expand/pallas_call | solution.py:255
  149.7 2.3 collective-permute-start.27
  151.9 7.8 %collective-permute-done.35 = bf16[2,320,640]{2,1,0:T(8,128)(2,1)S(1)} collective-permute-done((bf16[2,320,640]{2,1,0:T(8,128)(2,1)S(1)}, bf16[2,320,640]{2,1,0:T(8,128)(2,1)S(1)}, u32[]{:S(2)}, u32[]{:S(2)}) %collective-permute-start.35) | collective-permute-done | bytes 819232 | tf_op jit(solution)/shard_map/ppermute | solution.py:31
  161.7 26.0 %collective-permute-done.17 = bf16[320,640]{1,0:T(8,128)(2,1)S(1)} collective-permute-done((bf16[320,640]{1,0:T(8,128)(2,1)S(1)}, bf16[320,640]{1,0:T(8,128)(2,1)S(1)}, u32[]{:S(2)}, u32[]{:S(2)}) %collective-permute-start.17) | collective-permute-done | bytes 409632 | tf_op jit(solution)/shard_map/ppermute | solution.py:31
  189.4 2.7 %collective-permute-done.27 = bf16[320,640]{1,0:T(8,128)(2,1)S(1)} collective-permute-done((bf16[320,640]{1,0:T(8,128)(2,1)S(1)}, bf16[320,640]{1,0:T(8,128)(2,1)S(1)}, u32[]{:S(2)}, u32[]{:S(2)}) %collective-permute-start.27) | collective-permute-done | bytes 409632 | tf_op jit(solution)/shard_map/ppermute | solution.py:31
  193.8 4.4 %collective-permute-done.36 = bf16[320,640]{1,0:T(8,128)(2,1)S(1)} collective-permute-done((bf16[320,640]{1,0:T(8,128)(2,1)S(1)}, bf16[320,640]{1,0:T(8,128)(2,1)S(1)}, u32[]{:S(2)}, u32[]{:S(2)}) %collective-permute-start.36) | collective-permute-done | bytes 409632 | tf_op jit(solution)/shard_map/ppermute | solution.py:31
  201.7 2.7 %collective-permute-done.19.refs_2_.refs_7_ = bf16[320,640]{1,0:T(8,128)(2,1)S(1)} collective-permute-done((bf16[320,640]{1,0:T(8,128)(2,1)S(1)}, bf16[320,640]{1,0:T(8,128)(2,1)S(1)}, u32[]{:S(2)}, u32[]{:S(2)}) %collective-permute-start.19) | collective-permute-done | bytes 409632 | tf_op jit(solution)/shard_map/ppermute | solution.py:31
  207.8 5.2 %collective-permute-done.29.refs_2_.refs_12_ = bf16[320,640]{1,0:T(8,128)(2,1)S(1)} collective-permute-done((bf16[320,640]{1,0:T(8,128)(2,1)S(1)}, bf16[320,640]{1,0:T(8,128)(2,1)S(1)}, u32[]{:S(2)}, u32[]{:S(2)}) %collective-permute-start.29) | collective-permute-done | bytes 409632 | tf_op jit(solution)/shard_map/ppermute | solution.py:31
  213.1 7.3 %collective-permute-done.38.refs_2_.refs_17_ = bf16[320,640]{1,0:T(8,128)(2,1)S(1)} collective-permute-done((bf16[320,640]{1,0:T(8,128)(2,1)S(1)}, bf16[320,640]{1,0:T(8,128)(2,1)S(1)}, u32[]{:S(2)}, u32[]{:S(2)}) %collective-permute-start.38) | collective-permute-done | bytes 409632 | tf_op jit(solution)/shard_map/ppermute | solution.py:31
  221.1 2.1 collective-permute-start.30
  236.1 5.5 %collective-permute-done.45.refs_1_.refs_21_ = bf16[160,640]{1,0:T(8,128)(2,1)S(1)} collective-permute-done((bf16[160,640]{1,0:T(8,128)(2,1)S(1)}, bf16[160,640]{1,0:T(8,128)(2,1)S(1)}, u32[]{:S(2)}, u32[]{:S(2)}) %collective-permute-start.45) | collective-permute-done | bytes 204832 | tf_op jit(solution)/shard_map/ppermute | solution.py:31
  243.7 2.6 collective-permute-done.9.refs_3_
  248.7 2.2 collective-permute-done.47.refs_3_.refs_23_
  254.8 9.1 %mix.1 = f32[2,320,2560]{2,1,0:T(8,128)} custom-call(s32[6]{0:T(128)} %stack.46.info_ref, f32[2,4]{1,0:T(2,128)} %w_ref.1, bf16[160,640]{1,0:T(8,128)(2,1)} %copy-done.12, bf16[160,640]{1,0:T(8,128)(2,1)} %copy-done.14, bf16[160,640]{1,0:T(8,128)(2,1)} %copy-done.15, bf16[80,640]{1,0:T(8,128)(2,1)} %copy-done.24, bf16[80,640]{1,0:T(8,128)(2,1)} %copy-done.25, ...), custom_call_target="tpu_custom_call" | custom-call | tf_op jit(solution)/shard_map/mix/pallas_call | solution.py:385
  (176 shorter events, 63.6 us)
Async XLA Ops:
  0.0 76.4 %collective-permute-start.3 = (bf16[512,4096]{1,0:T(8,128)(2,1)}, bf16[512,4096]{1,0:T(8,128)(2,1)}, u32[]{:S(2)}, u32[]{:S(2)}) collective-permute-start(bf16[512,4096]{1,0:T(8,128)(2,1)} %bitcast.40), channel_id=1, source_target_pairs={{0,1},{1,0},{2,3},{3,2},{4,5},{5,4},{6,7},{7,6},{8,9},{9,8},{10,11... | collective-permute-start | bytes 12582920 | tf_op jit(solution)/shard_map/ppermute | solution.py:31
  2.2 20.1 %collective-permute-start = (bf16[80,4096]{1,0:T(8,128)(2,1)}, bf16[80,4096]{1,0:T(8,128)(2,1)S(1)}, u32[]{:S(2)}, u32[]{:S(2)}) collective-permute-start(bf16[80,4096]{1,0:T(8,128)(2,1)} %refs_1_.1), channel_id=1, source_target_pairs={{0,2},{1,3},{2,0},{3,1},{4,6},{5,7},{6,4},{7,5},{8,10},{9,11},{10,... | collective-permute-start | bytes 1966088 | tf_op jit(solution)/shard_map/ppermute | solution.py:31
  6.7 30.1 %collective-permute-start.2 = (bf16[80,4096]{1,0:T(8,128)(2,1)S(1)}, bf16[80,4096]{1,0:T(8,128)(2,1)}, u32[]{:S(2)}, u32[]{:S(2)}) collective-permute-start(bf16[80,4096]{1,0:T(8,128)(2,1)S(1)} %collective-permute-done.1), channel_id=1, source_target_pairs={{0,2},{1,3},{2,0},{3,1},{4,6},{5,7},{6,4},{7,5},{8,10},{9,11},{10,... | collective-permute-start | bytes 1966088 | tf_op jit(solution)/shard_map/ppermute | solution.py:31
  23.8 18.9 %collective-permute-start.13 = (bf16[80,4096]{1,0:T(8,128)(2,1)}, bf16[80,4096]{1,0:T(8,128)(2,1)S(1)}, u32[]{:S(2)}, u32[]{:S(2)}) collective-permute-start(bf16[80,4096]{1,0:T(8,128)(2,1)} %refs_1_.1), channel_id=1, source_target_pairs={{0,8},{1,9},{2,10},{3,11},{4,12},{5,13},{6,14},{7,15},{8,0},{9,1},... | collective-permute-start | bytes 1966088 | tf_op jit(solution)/shard_map/ppermute | solution.py:31
  25.3 31.4 %collective-permute-start.22 = (bf16[80,4096]{1,0:T(8,128)(2,1)}, bf16[80,4096]{1,0:T(8,128)(2,1)S(1)}, u32[]{:S(2)}, u32[]{:S(2)}) collective-permute-start(bf16[80,4096]{1,0:T(8,128)(2,1)} %refs_1_.1), channel_id=1, source_target_pairs={{0,16},{1,17},{2,18},{3,19},{4,20},{5,21},{6,22},{7,23},{8,24},{9,... | collective-permute-start | bytes 1966088 | tf_op jit(solution)/shard_map/ppermute | solution.py:31
  36.8 38.8 %collective-permute-start.4 = (bf16[2560,512]{1,0:T(8,128)(2,1)}, bf16[2560,512]{1,0:T(8,128)(2,1)S(1)}, u32[]{:S(2)}, u32[]{:S(2)}) collective-permute-start(bf16[2560,512]{1,0:T(8,128)(2,1)} %own_ref.9), channel_id=1, source_target_pairs={{0,1},{1,0},{2,3},{3,2},{4,5},{5,4},{6,7},{7,6},{8,9},{9,8},{10,11... | collective-permute-start | bytes 7864328 | tf_op jit(solution)/shard_map/ppermute | solution.py:31
  36.8 18.2 %collective-permute-start.12 = (bf16[80,4096]{1,0:T(8,128)(2,1)}, bf16[80,4096]{1,0:T(8,128)(2,1)S(1)}, u32[]{:S(2)}, u32[]{:S(2)}) collective-permute-start(bf16[80,4096]{1,0:T(8,128)(2,1)} %collective-permute-done.11), channel_id=1, source_target_pairs={{0,2},{1,3},{2,0},{3,1},{4,6},{5,7},{6,4},{7,5},{8,10},{9,11},{10,... | collective-permute-start | bytes 1966088 | tf_op jit(solution)/shard_map/ppermute | solution.py:31
  42.7 15.5 %collective-permute-start.14 = (bf16[80,4096]{1,0:T(8,128)(2,1)S(1)}, bf16[80,4096]{1,0:T(8,128)(2,1)S(1)}, u32[]{:S(2)}, u32[]{:S(2)}) collective-permute-start(bf16[80,4096]{1,0:T(8,128)(2,1)S(1)} %collective-permute-done.refs_1_.refs_0_), channel_id=1, source_target_pairs={{0,8},{1,9},{2,10},{3,11},{4,12},{5,13},{6,14},{7,15},{8,0},{9,1},... | collective-permute-start | bytes 1966088 | tf_op jit(solution)/shard_map/ppermute | solution.py:31
  55.0 17.6 %collective-permute-start.23 = (bf16[80,4096]{1,0:T(8,128)(2,1)S(1)}, bf16[80,4096]{1,0:T(8,128)(2,1)S(1)}, u32[]{:S(2)}, u32[]{:S(2)}) collective-permute-start(bf16[80,4096]{1,0:T(8,128)(2,1)S(1)} %collective-permute-done.refs_1_.refs_0_), channel_id=1, source_target_pairs={{0,16},{1,17},{2,18},{3,19},{4,20},{5,21},{6,22},{7,23},{8,24},{9,... | collective-permute-start | bytes 1966088 | tf_op jit(solution)/shard_map/ppermute | solution.py:31
  56.6 17.6 %collective-permute-start.15 = (bf16[80,4096]{1,0:T(8,128)(2,1)S(1)}, bf16[80,4096]{1,0:T(8,128)(2,1)S(1)}, u32[]{:S(2)}, u32[]{:S(2)}) collective-permute-start(bf16[80,4096]{1,0:T(8,128)(2,1)S(1)} %broadcast_select_fusion.3.refs_2_), channel_id=1, source_target_pairs={{0,8},{1,9},{2,10},{3,11},{4,12},{5,13},{6,14},{7,15},{8,0},{9,1},... | collective-permute-start | bytes 1966088 | tf_op jit(solution)/shard_map/ppermute | solution.py:31
  58.2 29.7 %collective-permute-start.24 = (bf16[80,4096]{1,0:T(8,128)(2,1)S(1)}, bf16[80,4096]{1,0:T(8,128)(2,1)S(1)}, u32[]{:S(2)}, u32[]{:S(2)}) collective-permute-start(bf16[80,4096]{1,0:T(8,128)(2,1)S(1)} %broadcast_select_fusion.3.refs_2_), channel_id=1, source_target_pairs={{0,16},{1,17},{2,18},{3,19},{4,20},{5,21},{6,22},{7,23},{8,24},{9,... | collective-permute-start | bytes 1966088 | tf_op jit(solution)/shard_map/ppermute | solution.py:31
  72.6 17.6 %collective-permute-start.25 = (bf16[80,4096]{1,0:T(8,128)(2,1)S(1)}, bf16[80,4096]{1,0:T(8,128)(2,1)S(1)}, u32[]{:S(2)}, u32[]{:S(2)}) collective-permute-start(bf16[80,4096]{1,0:T(8,128)(2,1)S(1)} %broadcast_select_fusion.2.refs_2_), channel_id=1, source_target_pairs={{0,8},{1,9},{2,10},{3,11},{4,12},{5,13},{6,14},{7,15},{8,0},{9,1},... | collective-permute-start | bytes 1966088 | tf_op jit(solution)/shard_map/ppermute | solution.py:31
  74.2 30.0 %collective-permute-start.33 = (bf16[80,4096]{1,0:T(8,128)(2,1)S(1)}, bf16[80,4096]{1,0:T(8,128)(2,1)S(1)}, u32[]{:S(2)}, u32[]{:S(2)}) collective-permute-start(bf16[80,4096]{1,0:T(8,128)(2,1)S(1)} %get-tuple-element.26), channel_id=1, source_target_pairs={{0,8},{1,9},{2,10},{3,11},{4,12},{5,13},{6,14},{7,15},{8,0},{9,1},... | collective-permute-start | bytes 1966088 | tf_op jit(solution)/shard_map/ppermute | solution.py:31
  75.6 34.0 %collective-permute-start.32 = (bf16[80,4096]{1,0:T(8,128)(2,1)S(1)}, bf16[80,4096]{1,0:T(8,128)(2,1)S(1)}, u32[]{:S(2)}, u32[]{:S(2)}) collective-permute-start(bf16[80,4096]{1,0:T(8,128)(2,1)S(1)} %broadcast_select_fusion.2.refs_2_), channel_id=1, source_target_pairs={{0,16},{1,17},{2,18},{3,19},{4,20},{5,21},{6,22},{7,23},{8,24},{9,... | collective-permute-start | bytes 1966088 | tf_op jit(solution)/shard_map/ppermute | solution.py:31
  76.4 38.4 %collective-permute-start.34 = (bf16[80,4096]{1,0:T(8,128)(2,1)S(1)}, bf16[80,4096]{1,0:T(8,128)(2,1)S(1)}, u32[]{:S(2)}, u32[]{:S(2)}) collective-permute-start(bf16[80,4096]{1,0:T(8,128)(2,1)S(1)} %collective-permute-done.15.refs_5_), channel_id=1, source_target_pairs={{0,16},{1,17},{2,18},{3,19},{4,20},{5,21},{6,22},{7,23},{8,24},{9,... | collective-permute-start | bytes 1966088 | tf_op jit(solution)/shard_map/ppermute | solution.py:31
  87.9 48.2 %collective-permute-start.41 = (bf16[80,4096]{1,0:T(8,128)(2,1)S(1)}, bf16[80,4096]{1,0:T(8,128)(2,1)S(1)}, u32[]{:S(2)}, u32[]{:S(2)}) collective-permute-start(bf16[80,4096]{1,0:T(8,128)(2,1)S(1)} %get-tuple-element.25), channel_id=1, source_target_pairs={{0,8},{1,9},{2,10},{3,11},{4,12},{5,13},{6,14},{7,15},{8,0},{9,1},... | collective-permute-start | bytes 1966088 | tf_op jit(solution)/shard_map/ppermute | solution.py:31
  90.2 46.2 %collective-permute-start.42 = (bf16[80,4096]{1,0:T(8,128)(2,1)S(1)}, bf16[80,4096]{1,0:T(8,128)(2,1)S(1)}, u32[]{:S(2)}, u32[]{:S(2)}) collective-permute-start(bf16[80,4096]{1,0:T(8,128)(2,1)S(1)} %collective-permute-done.25.refs_5_), channel_id=1, source_target_pairs={{0,16},{1,17},{2,18},{3,19},{4,20},{5,21},{6,22},{7,23},{8,24},{9,... | collective-permute-start | bytes 1966088 | tf_op jit(solution)/shard_map/ppermute | solution.py:31
  104.3 43.5 %collective-permute-start.16 = (bf16[2,320,640]{2,1,0:T(8,128)(2,1)S(1)}, bf16[2,320,640]{2,1,0:T(8,128)(2,1)S(1)}, u32[]{:S(2)}, u32[]{:S(2)}) collective-permute-start(bf16[2,320,640]{2,1,0:T(8,128)(2,1)S(1)} %get-tuple-element.18), channel_id=1, source_target_pairs={{0,2},{1,3},{2,0},{3,1},{4,6},{5,7},{6,4},{7,5},{8,10},{9,11},{10,... | collective-permute-start | bytes 2457608 | tf_op jit(solution)/shard_map/ppermute | solution.py:31
  109.6 40.0 %collective-permute-start.26 = (bf16[2,320,640]{2,1,0:T(8,128)(2,1)S(1)}, bf16[2,320,640]{2,1,0:T(8,128)(2,1)S(1)}, u32[]{:S(2)}, u32[]{:S(2)}) collective-permute-start(bf16[2,320,640]{2,1,0:T(8,128)(2,1)S(1)} %get-tuple-element.20), channel_id=1, source_target_pairs={{0,2},{1,3},{2,0},{3,1},{4,6},{5,7},{6,4},{7,5},{8,10},{9,11},{10,... | collective-permute-start | bytes 2457608 | tf_op jit(solution)/shard_map/ppermute | solution.py:31
  125.0 34.8 %collective-permute-start.35 = (bf16[2,320,640]{2,1,0:T(8,128)(2,1)S(1)}, bf16[2,320,640]{2,1,0:T(8,128)(2,1)S(1)}, u32[]{:S(2)}, u32[]{:S(2)}) collective-permute-start(bf16[2,320,640]{2,1,0:T(8,128)(2,1)S(1)} %get-tuple-element.22), channel_id=1, source_target_pairs={{0,2},{1,3},{2,0},{3,1},{4,6},{5,7},{6,4},{7,5},{8,10},{9,11},{10,... | collective-permute-start | bytes 2457608 | tf_op jit(solution)/shard_map/ppermute | solution.py:31
  136.1 56.1 %collective-permute-start.5 = (bf16[2,160,640]{2,1,0:T(8,128)(2,1)S(1)}, bf16[2,160,640]{2,1,0:T(8,128)(2,1)S(1)}, u32[]{:S(2)}, u32[]{:S(2)}) collective-permute-start(bf16[2,160,640]{2,1,0:T(8,128)(2,1)S(1)} %get-tuple-element.16), channel_id=1, source_target_pairs={{0,2},{1,3},{2,0},{3,1},{4,6},{5,7},{6,4},{7,5},{8,10},{9,11},{10,... | collective-permute-start | bytes 1228808 | tf_op jit(solution)/shard_map/ppermute | solution.py:31
  145.9 58.6 %collective-permute-start.43 = (bf16[2,160,640]{2,1,0:T(8,128)(2,1)S(1)}, bf16[2,160,640]{2,1,0:T(8,128)(2,1)S(1)}, u32[]{:S(2)}, u32[]{:S(2)}) collective-permute-start(bf16[2,160,640]{2,1,0:T(8,128)(2,1)S(1)} %get-tuple-element.24), channel_id=1, source_target_pairs={{0,2},{1,3},{2,0},{3,1},{4,6},{5,7},{6,4},{7,5},{8,10},{9,11},{10,... | collective-permute-start | bytes 1228808 | tf_op jit(solution)/shard_map/ppermute | solution.py:31
  147.9 39.8 %collective-permute-start.17 = (bf16[320,640]{1,0:T(8,128)(2,1)S(1)}, bf16[320,640]{1,0:T(8,128)(2,1)S(1)}, u32[]{:S(2)}, u32[]{:S(2)}) collective-permute-start(bf16[320,640]{1,0:T(8,128)(2,1)S(1)} %fusion.3), channel_id=1, source_target_pairs={{0,6},{1,7},{2,4},{3,5},{4,2},{5,3},{6,0},{7,1},{8,14},{9,15},{10,... | collective-permute-start | bytes 1228808 | tf_op jit(solution)/shard_map/ppermute | solution.py:31
  149.7 42.4 %collective-permute-start.27 = (bf16[320,640]{1,0:T(8,128)(2,1)S(1)}, bf16[320,640]{1,0:T(8,128)(2,1)S(1)}, u32[]{:S(2)}, u32[]{:S(2)}) collective-permute-start(bf16[320,640]{1,0:T(8,128)(2,1)S(1)} %fusion.4), channel_id=1, source_target_pairs={{0,6},{1,7},{2,4},{3,5},{4,2},{5,3},{6,0},{7,1},{8,14},{9,15},{10,... | collective-permute-start | bytes 1228808 | tf_op jit(solution)/shard_map/ppermute | solution.py:31
  159.9 38.3 %collective-permute-start.36 = (bf16[320,640]{1,0:T(8,128)(2,1)S(1)}, bf16[320,640]{1,0:T(8,128)(2,1)S(1)}, u32[]{:S(2)}, u32[]{:S(2)}) collective-permute-start(bf16[320,640]{1,0:T(8,128)(2,1)S(1)} %fusion.5), channel_id=1, source_target_pairs={{0,6},{1,7},{2,4},{3,5},{4,2},{5,3},{6,0},{7,1},{8,14},{9,15},{10,... | collective-permute-start | bytes 1228808 | tf_op jit(solution)/shard_map/ppermute | solution.py:31
  200.2 20.9 %collective-permute-start.37 = (bf16[320,640]{1,0:T(8,128)(2,1)S(1)}, bf16[320,640]{1,0:T(8,128)(2,1)S(1)}, u32[]{:S(2)}, u32[]{:S(2)}) collective-permute-start(bf16[320,640]{1,0:T(8,128)(2,1)S(1)} %fusion.refs_0_.refs_15_), channel_id=1, source_target_pairs={{0,8},{1,9},{2,10},{3,11},{4,12},{5,13},{6,14},{7,15},{8,0},{9,1},... | collective-permute-start | bytes 1228808 | tf_op jit(solution)/shard_map/ppermute | solution.py:31
  204.4 16.0 %collective-permute-start.38 = (bf16[320,640]{1,0:T(8,128)(2,1)S(1)}, bf16[320,640]{1,0:T(8,128)(2,1)S(1)}, u32[]{:S(2)}, u32[]{:S(2)}) collective-permute-start(bf16[320,640]{1,0:T(8,128)(2,1)S(1)} %fusion.refs_0_.refs_15_), channel_id=1, source_target_pairs={{0,16},{1,17},{2,18},{3,19},{4,20},{5,21},{6,22},{7,23},{8,24},{9,... | collective-permute-start | bytes 1228808 | tf_op jit(solution)/shard_map/ppermute | solution.py:31
  204.5 18.8 %collective-permute-start.6 = (bf16[160,640]{1,0:T(8,128)(2,1)S(1)}, bf16[160,640]{1,0:T(8,128)(2,1)S(1)}, u32[]{:S(2)}, u32[]{:S(2)}) collective-permute-start(bf16[160,640]{1,0:T(8,128)(2,1)S(1)} %fusion.8), channel_id=1, source_target_pairs={{0,6},{1,7},{2,4},{3,5},{4,2},{5,3},{6,0},{7,1},{8,14},{9,15},{10,... | collective-permute-start | bytes 614408 | tf_op jit(solution)/shard_map/ppermute | solution.py:31
  206.3 17.3 %collective-permute-start.20 = (bf16[160,640]{1,0:T(8,128)(2,1)S(1)}, bf16[160,640]{1,0:T(8,128)(2,1)S(1)}, u32[]{:S(2)}, u32[]{:S(2)}) collective-permute-start(bf16[160,640]{1,0:T(8,128)(2,1)S(1)} %slice.126), channel_id=1, source_target_pairs={{0,8},{1,9},{2,10},{3,11},{4,12},{5,13},{6,14},{7,15},{8,0},{9,1},... | collective-permute-start | bytes 614408 | tf_op jit(solution)/shard_map/ppermute | solution.py:31
  231.5 22.2 %collective-permute-start.50 = (bf16[4,320,384]{2,1,0:T(8,128)(2,1)}, bf16[4,320,384]{2,1,0:T(8,128)(2,1)}, u32[]{:S(2)}, u32[]{:S(2)}) collective-permute-start(bf16[4,320,384]{2,1,0:T(8,128)(2,1)} %hand_over.6), channel_id=1, source_target_pairs={{0,1},{1,0},{2,3},{3,2},{4,5},{5,4},{6,7},{7,6},{8,9},{9,8},{10,11... | collective-permute-start | bytes 2949128 | tf_op jit(solution)/shard_map/ppermute | solution.py:31
  231.6 22.2 %collective-permute-start.51 = (bf16[4,320,384]{2,1,0:T(8,128)(2,1)}, bf16[4,320,384]{2,1,0:T(8,128)(2,1)}, u32[]{:S(2)}, u32[]{:S(2)}) collective-permute-start(bf16[4,320,384]{2,1,0:T(8,128)(2,1)} %hand_over.7), channel_id=1, source_target_pairs={{0,1},{1,0},{2,3},{3,2},{4,5},{5,4},{6,7},{7,6},{8,9},{9,8},{10,11... | collective-permute-start | bytes 2949128 | tf_op jit(solution)/shard_map/ppermute | solution.py:31
  233.9 19.9 %collective-permute-start.52 = (bf16[4,320,384]{2,1,0:T(8,128)(2,1)}, bf16[4,320,384]{2,1,0:T(8,128)(2,1)S(1)}, u32[]{:S(2)}, u32[]{:S(2)}) collective-permute-start(bf16[4,320,384]{2,1,0:T(8,128)(2,1)} %hand_over.8), channel_id=1, source_target_pairs={{0,1},{1,0},{2,3},{3,2},{4,5},{5,4},{6,7},{7,6},{8,9},{9,8},{10,11... | collective-permute-start | bytes 2949128 | tf_op jit(solution)/shard_map/ppermute | solution.py:31
  (51 other events, 780.0 us)

commit v2 on v1

--- a/solution.py
+++ b/solution.py
@@ -176,7 +176,7 @@
     c = 2 * n * h
 
     def kernel(inner_ref, *refs):
-        e, (own_ref, far_ref, out_ref, lhs) = refs[: 3 * n], refs[3 * n :]
+        e, (own_ref, far_ref, out_ref, lhs, sems) = refs[: 3 * n], refs[3 * n :]
         step = pl.program_id(0)
 
         @pl.when(step == 0)
@@ -186,20 +186,23 @@
 
                 low = pl.ds(pl.multiple_of(2 * u * h + inner_ref[1] * h, PACK), h)
                 high = pl.ds(pl.multiple_of((2 * u + 1) * h - inner_ref[1] * h, PACK), h)
-
                 if a is b:
-                    lhs[low, :] = a[...]
+                    pltpu.make_async_copy(a, lhs.at[low], sems.at[2 * u]).start()
                 else:
 
                     @pl.when(inner_ref[0] == 1)
                     def _():
-                        lhs[low, :] = a[...]
+                        pltpu.make_async_copy(a, lhs.at[low], sems.at[2 * u]).start()
 
                     @pl.when(inner_ref[0] == 0)
                     def _():
-                        lhs[low, :] = b[...]
-
-                lhs[high, :] = third[...]
+                        pltpu.make_async_copy(b, lhs.at[low], sems.at[2 * u]).start()
+
+                pltpu.make_async_copy(third, lhs.at[high], sems.at[2 * u + 1]).start()
+            for u in range(n):
+                for part in range(2):
+                    rows = pl.ds((2 * u + part) * h, h)
+                    pltpu.make_async_copy(e[3 * u], lhs.at[rows], sems.at[2 * u + part]).wait()
 
         @pl.when(step < steps)
         def _():
@@ -214,16 +217,16 @@
         grid_spec=pltpu.PrefetchScalarGridSpec(
             num_scalar_prefetch=1,
             grid=(2 * steps,),
-            in_specs=[pl.BlockSpec((h, depth), lambda i, s: (0, 0), pipeline_mode=pl.Buffered(1))] * len(flat)
+            in_specs=[pl.BlockSpec(memory_space=pl.ANY)] * len(flat)
             + [
                 pl.BlockSpec((tile, depth), lambda i, s: (jnp.minimum(i, steps - 1), 0)),
                 pl.BlockSpec((tile, depth), lambda i, s: (jnp.maximum(i - steps, 0), 0)),
             ],
             out_specs=pl.BlockSpec((c, tile), lambda i, s: (0, i)),
-            scratch_shapes=[pltpu.VMEM((c, depth), jnp.bfloat16)],
+            scratch_shapes=[pltpu.VMEM((c, depth), jnp.bfloat16), pltpu.SemaphoreType.DMA((2 * n,))],
         ),
         out_shape=jax.ShapeDtypeStruct((c, 2 * held), jnp.bfloat16),
-        compiler_params=pltpu.CompilerParams(vmem_limit_bytes=22 << 20, dimension_semantics=("arbitrary",)),
+        compiler_params=pltpu.CompilerParams(vmem_limit_bytes=20 << 20, dimension_semantics=("arbitrary",)),
         cost_estimate=pl.CostEstimate(
             flops=4 * c * depth * held,
             bytes_accessed=2 * (c * depth + 2 * held * depth + 2 * c * held),
@@ -458,16 +461,19 @@
     f32 = jnp.float32
 
     kept, given = [], []
-    for piece in PIECES:
+    for i, piece in enumerate(PIECES):
         near = project([unit(*u) for u in piece], h, place, mine, theirs)
         give, keep = expand(order, near, outs, chip_rows)
         got = pair(give)
         last = mirror((keep[1].astype(f32) + got[1].astype(f32)).astype(jnp.bfloat16))
         expanded = (keep[0].astype(f32) + got[0].astype(f32) + last.astype(f32)).astype(jnp.bfloat16)
         from_x, from_y = over_x(expanded), over_y(expanded)
-        cut = expanded.shape[0] // 2
-        low, high = over_x(from_y[:cut]), over_y(from_x[cut:])
-        spread = [expanded, from_x, from_y, low, high]
+        if i < len(PIECES) - 2:
+            diagonal = [over_x(from_y) if i % 2 == 0 else over_y(from_x)]
+        else:
+            cut = expanded.shape[0] // 2
+            diagonal = [over_x(from_y[:cut]), over_y(from_x[cut:])]
+        spread = [expanded, from_x, from_y, *diagonal]
         start = ints(jnp.where(core == 0, first // LANES, 0))
         give = hand_over(start, spread, [part.shape[0] for part in spread], window)
         kept.append(spread)

time: 265 us -> 292 us (1.10)
  waiting for transfers between devices: 115 us -> 153 us
  starting transfers between devices: 79.8 us -> 56.8 us
  Pallas kernels: 64.6 us -> 71.3 us
  local copies, waits for them, and re-layouts: 1.89 us -> 7.67 us
    ppermute x54 -> x51, waiting for transfers between devices: 115 us -> 153 us  [send(): return lax.ppermute(value, AXES, pairs)]
    ppermute x54 -> x51, starting transfers between devices: 79.8 us -> 56.8 us  [send(): return lax.ppermute(value, AXES, pairs)]
    unnamed x58 -> x50, local copies, waits for them, and re-layouts: 1.08 us -> 6.04 us
    pallas_call x5, Pallas kernels: 6.1 us -> 10 us  [hand_over(): pl.pallas_call(kernel, grid_spec=pltpu.PrefetchScalarGridSpec(num_scalar_...]
  transfers between devices with their start and end apart: 54 -> 51, of which waited for: 21 -> 22; matrix products, arithmetic and copies ran while one was open for 1% -> 1% of each run, Pallas kernels for 21% -> 21%
where the time goes in v2:
time: 292 us; the launch traced here: 291 us
  waiting for transfers between devices  153 us (52%)
  Pallas kernels  71.3 us (24%)
  starting transfers between devices  56.8 us (19%)
  local copies, waits for them, and re-layouts  7.67 us (3%)
    ppermute x51, waiting for transfers between devices, send(): return lax.ppermute(value, AXES, pairs)  153 us
    ppermute x51, starting transfers between devices, send(): return lax.ppermute(value, AXES, pairs)  56.8 us
    pallas_call x5, Pallas kernels, project(): pl.pallas_call(kernel, grid_spec=pltpu.PrefetchScalarGridSpec(num_scalar_...  35.6 us
    pallas_call x5, Pallas kernels, expand(): pl.pallas_call(kernel, grid_spec=pltpu.PrefetchScalarGridSpec(num_scalar_...  16.6 us
    pallas_call x5, Pallas kernels, hand_over(): pl.pallas_call(kernel, grid_spec=pltpu.PrefetchScalarGridSpec(num_scalar_...  10 us
    pallas_call x1, Pallas kernels, mix(): pl.pallas_call(kernel, grid_spec=pltpu.PrefetchScalarGridSpec(num_scalar_...  9.14 us
    unnamed x50, local copies, waits for them, and re-layouts  6.04 us
  transfers between devices with their start and end apart: 51, of which 22 were waited for; matrix products, arithmetic and copies ran while one was open for 1% of the time, Pallas kernels for 21%

profile of v2, /device:TPU:0, one launch (start us, length us, event | category | flops | bytes accessed | tf_op | source)
XLA Modules:
  0.0 291.1 jit_solution(3553607087123075701)
XLA Ops:
  3.1 6.5 %collective-permute-start.1 = (bf16[80,4096]{1,0:T(8,128)(2,1)}, bf16[80,4096]{1,0:T(8,128)(2,1)}, u32[]{:S(2)}, u32[]{:S(2)}) collective-permute-start(bf16[80,4096]{1,0:T(8,128)(2,1)} %refs_1_.1), channel_id=1, source_target_pairs={{0,0},{1,1},{2,4},{3,5},{4,2},{5,3},{6,6},{7,7},{8,8},{9,9},{10,12... | collective-permute-start | bytes 1966088 | tf_op jit(solution)/shard_map/ppermute | solution.py:31
  11.2 7.5 %collective-permute-done.refs_1_.refs_0_ = bf16[80,4096]{1,0:T(8,128)(2,1)S(1)} collective-permute-done((bf16[80,4096]{1,0:T(8,128)(2,1)}, bf16[80,4096]{1,0:T(8,128)(2,1)S(1)}, u32[]{:S(2)}, u32[]{:S(2)}) %collective-permute-start) | collective-permute-done | bytes 655392 | tf_op jit(solution)/shard_map/ppermute | solution.py:31
  22.0 5.5 %collective-permute-done.20.refs_0_.refs_1_ = bf16[80,4096]{1,0:T(8,128)(2,1)S(1)} collective-permute-done((bf16[80,4096]{1,0:T(8,128)(2,1)}, bf16[80,4096]{1,0:T(8,128)(2,1)S(1)}, u32[]{:S(2)}, u32[]{:S(2)}) %collective-permute-start.20) | collective-permute-done | bytes 655392 | tf_op jit(solution)/shard_map/ppermute | solution.py:31
  28.2 12.5 %collective-permute-done.21.refs_1_.refs_0_ = bf16[80,4096]{1,0:T(8,128)(2,1)S(1)} collective-permute-done((bf16[80,4096]{1,0:T(8,128)(2,1)S(1)}, bf16[80,4096]{1,0:T(8,128)(2,1)S(1)}, u32[]{:S(2)}, u32[]{:S(2)}) %collective-permute-start.21) | collective-permute-done | bytes 655392 | tf_op jit(solution)/shard_map/ppermute | solution.py:31
  40.8 16.1 %collective-permute-done.2 = bf16[80,4096]{1,0:T(8,128)(2,1)S(1)} collective-permute-done((bf16[80,4096]{1,0:T(8,128)(2,1)}, bf16[80,4096]{1,0:T(8,128)(2,1)S(1)}, u32[]{:S(2)}, u32[]{:S(2)}) %collective-permute-start.2) | collective-permute-done | bytes 655392 | tf_op jit(solution)/shard_map/ppermute | solution.py:31
  58.7 14.4 %collective-permute-done.11 = bf16[80,4096]{1,0:T(8,128)(2,1)S(1)} collective-permute-done((bf16[80,4096]{1,0:T(8,128)(2,1)S(1)}, bf16[80,4096]{1,0:T(8,128)(2,1)S(1)}, u32[]{:S(2)}, u32[]{:S(2)}) %collective-permute-start.11) | collective-permute-done | bytes 655392 | tf_op jit(solution)/shard_map/ppermute | solution.py:31
  75.9 14.9 %collective-permute-done.14.refs_5_ = bf16[80,4096]{1,0:T(8,128)(2,1)S(1)} collective-permute-done((bf16[80,4096]{1,0:T(8,128)(2,1)S(1)}, bf16[80,4096]{1,0:T(8,128)(2,1)S(1)}, u32[]{:S(2)}, u32[]{:S(2)}) %collective-permute-start.14) | collective-permute-done | bytes 655392 | tf_op jit(solution)/shard_map/ppermute | solution.py:31
  92.9 7.3 %project.6.near_ref = bf16[320,1024]{1,0:T(8,128)(2,1)S(1)} custom-call(s32[2]{0:T(128)S(1)} %add_convert_fusion.5.inner_ref, bf16[80,4096]{1,0:T(8,128)(2,1)S(1)} %collective-permute-done.refs_1_.refs_0_, bf16[80,4096]{1,0:T(8,128)(2,1)S(1)} %copy-done.5, bf16[80,4096]{1,0:T(8,128)(2,1)S(1)} %broadcast_select_fusion.2.refs_2_, ...), custom_call_target="tpu_custom_call" | custom-call | flops 2684354560 | bytes 11665408 | tf_op jit(solution)/shard_map/project/pallas_call | solution.py:215
  101.8 6.8 %project.5.near_ref = bf16[160,1024]{1,0:T(8,128)(2,1)S(1)} custom-call(s32[2]{0:T(128)S(1)} %add_convert_fusion.5.inner_ref, bf16[80,4096]{1,0:T(8,128)(2,1)S(1)} %copy-done.5, bf16[80,4096]{1,0:T(8,128)(2,1)S(1)} %collective-permute-done.refs_1_.refs_0_, bf16[80,4096]{1,0:T(8,128)(2,1)S(1)} %broadcast_select_fusion.3.refs_2_, ...), custom_call_target="tpu_custom_call" | custom-call | flops 1342177280 | bytes 10027008 | tf_op jit(solution)/shard_map/project/pallas_call | solution.py:215
  108.6 2.9 expand.5
  111.5 3.6 %expand.6 = (bf16[2,320,640]{2,1,0:T(8,128)(2,1)S(1)}, bf16[2,320,640]{2,1,0:T(8,128)(2,1)S(1)}) custom-call(s32[4]{0:T(128)S(1)} %pad_add_fusion.order_ref, bf16[320,1024]{1,0:T(8,128)(2,1)S(1)} %project.6.near_ref, bf16[2560,512]{1,0:T(8,128)(2,1)S(1)} %copy-done.1, bf16[2560,512]{1,0:T(8,128)(2,1)S(1)} %collective-permute-done.4.far_ref), custom_call_target="tpu_custom_call" | custom-call | flops 1677721600 | bytes 7536640 | tf_op jit(solution)/shard_map/expand/pallas_call | solution.py:258
  115.7 3.2 %collective-permute-done.23.refs_5_ = bf16[80,4096]{1,0:T(8,128)(2,1)S(1)} collective-permute-done((bf16[80,4096]{1,0:T(8,128)(2,1)S(1)}, bf16[80,4096]{1,0:T(8,128)(2,1)S(1)}, u32[]{:S(2)}, u32[]{:S(2)}) %collective-permute-start.23) | collective-permute-done | bytes 655392 | tf_op jit(solution)/shard_map/ppermute | solution.py:31
  123.0 7.3 %project.8.near_ref = bf16[320,1024]{1,0:T(8,128)(2,1)S(1)} custom-call(s32[2]{0:T(128)S(1)} %add_convert_fusion.5.inner_ref, bf16[80,4096]{1,0:T(8,128)(2,1)S(1)} %collective-permute-done.21.refs_1_.refs_0_, bf16[80,4096]{1,0:T(8,128)(2,1)S(1)} %collective-permute-done.20.refs_0_.refs_1_, bf16[80,4096]{1,0:T(8,128)(2,1)S(1)} %collective-permute-done.29.refs_2_, ...), custom_call_target="tpu_custom_call" | custom-call | flops 2684354560 | bytes 11665408 | tf_op jit(solution)/shard_map/project/pallas_call | solution.py:215
  130.3 3.6 %expand.8 = (bf16[2,320,640]{2,1,0:T(8,128)(2,1)S(1)}, bf16[2,320,640]{2,1,0:T(8,128)(2,1)S(1)}) custom-call(s32[4]{0:T(128)S(1)} %pad_add_fusion.order_ref, bf16[320,1024]{1,0:T(8,128)(2,1)S(1)} %project.8.near_ref, bf16[2560,512]{1,0:T(8,128)(2,1)S(1)} %copy-done.1, bf16[2560,512]{1,0:T(8,128)(2,1)S(1)} %collective-permute-done.4.far_ref), custom_call_target="tpu_custom_call" | custom-call | flops 1677721600 | bytes 7536640 | tf_op jit(solution)/shard_map/expand/pallas_call | solution.py:258
  136.5 7.3 %project.7.near_ref = bf16[320,1024]{1,0:T(8,128)(2,1)S(1)} custom-call(s32[2]{0:T(128)S(1)} %add_convert_fusion.5.inner_ref, bf16[80,4096]{1,0:T(8,128)(2,1)S(1)} %collective-permute-done.20.refs_0_.refs_1_, bf16[80,4096]{1,0:T(8,128)(2,1)S(1)} %collective-permute-done.21.refs_1_.refs_0_, bf16[80,4096]{1,0:T(8,128)(2,1)S(1)} %collective-permute-done.22.refs_2_, ...), custom_call_target="tpu_custom_call" | custom-call | flops 2684354560 | bytes 11665408 | tf_op jit(solution)/shard_map/project/pallas_call | solution.py:215
  143.8 3.6 %expand.7 = (bf16[2,320,640]{2,1,0:T(8,128)(2,1)S(1)}, bf16[2,320,640]{2,1,0:T(8,128)(2,1)S(1)}) custom-call(s32[4]{0:T(128)S(1)} %pad_add_fusion.order_ref, bf16[320,1024]{1,0:T(8,128)(2,1)S(1)} %project.7.near_ref, bf16[2560,512]{1,0:T(8,128)(2,1)S(1)} %copy-done.1, bf16[2560,512]{1,0:T(8,128)(2,1)S(1)} %collective-permute-done.4.far_ref), custom_call_target="tpu_custom_call" | custom-call | flops 1677721600 | bytes 7536640 | tf_op jit(solution)/shard_map/expand/pallas_call | solution.py:258
  148.4 6.8 %project.9.near_ref = bf16[160,1024]{1,0:T(8,128)(2,1)S(1)} custom-call(s32[2]{0:T(128)S(1)} %add_convert_fusion.5.inner_ref, bf16[80,4096]{1,0:T(8,128)(2,1)S(1)} %collective-permute-done.38.refs_0_.refs_1_, bf16[80,4096]{1,0:T(8,128)(2,1)S(1)} %collective-permute-done.38.refs_0_.refs_1_, bf16[80,4096]{1,0:T(8,128)(2,1)S(1)} %collective-permute-done.39.refs_2_, ...), custom_call_target="tpu_custom_call" | custom-call | flops 1342177280 | bytes 10027008 | tf_op jit(solution)/shard_map/project/pallas_call | solution.py:215
  155.2 3.0 %expand.9 = (bf16[2,160,640]{2,1,0:T(8,128)(2,1)S(1)}, bf16[2,160,640]{2,1,0:T(8,128)(2,1)S(1)}) custom-call(s32[4]{0:T(128)S(1)} %pad_add_fusion.order_ref, bf16[160,1024]{1,0:T(8,128)(2,1)S(1)} %project.9.near_ref, bf16[2560,512]{1,0:T(8,128)(2,1)S(1)} %copy-done.1, bf16[2560,512]{1,0:T(8,128)(2,1)S(1)} %collective-permute-done.4.far_ref), custom_call_target="tpu_custom_call" | custom-call | flops 838860800 | bytes 6389760 | tf_op jit(solution)/shard_map/expand/pallas_call | solution.py:258
  162.1 5.7 %collective-permute-done.32 = bf16[2,320,640]{2,1,0:T(8,128)(2,1)S(1)} collective-permute-done((bf16[2,320,640]{2,1,0:T(8,128)(2,1)S(1)}, bf16[2,320,640]{2,1,0:T(8,128)(2,1)S(1)}, u32[]{:S(2)}, u32[]{:S(2)}) %collective-permute-start.32) | collective-permute-done | bytes 819232 | tf_op jit(solution)/shard_map/ppermute | solution.py:31
  170.5 13.0 %collective-permute-done.24 = bf16[2,320,640]{2,1,0:T(8,128)(2,1)S(1)} collective-permute-done((bf16[2,320,640]{2,1,0:T(8,128)(2,1)S(1)}, bf16[2,320,640]{2,1,0:T(8,128)(2,1)S(1)}, u32[]{:S(2)}, u32[]{:S(2)}) %collective-permute-start.24) | collective-permute-done | bytes 819232 | tf_op jit(solution)/shard_map/ppermute | solution.py:31
  183.6 3.4 %collective-permute-start.25 = (bf16[320,640]{1,0:T(8,128)(2,1)S(1)}, bf16[320,640]{1,0:T(8,128)(2,1)S(1)}, u32[]{:S(2)}, u32[]{:S(2)}) collective-permute-start(bf16[320,640]{1,0:T(8,128)(2,1)S(1)} %fusion.4), channel_id=1, source_target_pairs={{0,6},{1,7},{2,4},{3,5},{4,2},{5,3},{6,0},{7,1},{8,14},{9,15},{10,... | collective-permute-start | bytes 1228808 | tf_op jit(solution)/shard_map/ppermute | solution.py:31
  187.0 17.0 %collective-permute-done.16 = bf16[320,640]{1,0:T(8,128)(2,1)S(1)} collective-permute-done((bf16[320,640]{1,0:T(8,128)(2,1)S(1)}, bf16[320,640]{1,0:T(8,128)(2,1)S(1)}, u32[]{:S(2)}, u32[]{:S(2)}) %collective-permute-start.16) | collective-permute-done | bytes 409632 | tf_op jit(solution)/shard_map/ppermute | solution.py:31
  205.3 4.0 %collective-permute-done.33 = bf16[320,640]{1,0:T(8,128)(2,1)S(1)} collective-permute-done((bf16[320,640]{1,0:T(8,128)(2,1)S(1)}, bf16[320,640]{1,0:T(8,128)(2,1)S(1)}, u32[]{:S(2)}, u32[]{:S(2)}) %collective-permute-start.33) | collective-permute-done | bytes 409632 | tf_op jit(solution)/shard_map/ppermute | solution.py:31
  210.1 5.1 %collective-permute-done.25 = bf16[320,640]{1,0:T(8,128)(2,1)S(1)} collective-permute-done((bf16[320,640]{1,0:T(8,128)(2,1)S(1)}, bf16[320,640]{1,0:T(8,128)(2,1)S(1)}, u32[]{:S(2)}, u32[]{:S(2)}) %collective-permute-start.25) | collective-permute-done | bytes 409632 | tf_op jit(solution)/shard_map/ppermute | solution.py:31
  219.0 6.9 %collective-permute-done.35.refs_2_.refs_14_ = bf16[320,640]{1,0:T(8,128)(2,1)S(1)} collective-permute-done((bf16[320,640]{1,0:T(8,128)(2,1)S(1)}, bf16[320,640]{1,0:T(8,128)(2,1)S(1)}, u32[]{:S(2)}, u32[]{:S(2)}) %collective-permute-start.35) | collective-permute-done | bytes 409632 | tf_op jit(solution)/shard_map/ppermute | solution.py:31
  228.1 5.4 %collective-permute-done.41 = bf16[160,640]{1,0:T(8,128)(2,1)S(1)} collective-permute-done((bf16[160,640]{1,0:T(8,128)(2,1)S(1)}, bf16[160,640]{1,0:T(8,128)(2,1)S(1)}, u32[]{:S(2)}, u32[]{:S(2)}) %collective-permute-start.41) | collective-permute-done | bytes 204832 | tf_op jit(solution)/shard_map/ppermute | solution.py:31
  237.7 5.1 %collective-permute-done.36.refs_3_.refs_15_ = bf16[160,640]{1,0:T(8,128)(2,1)S(1)} collective-permute-done((bf16[160,640]{1,0:T(8,128)(2,1)S(1)}, bf16[160,640]{1,0:T(8,128)(2,1)S(1)}, u32[]{:S(2)}, u32[]{:S(2)}) %collective-permute-start.36) | collective-permute-done | bytes 204832 | tf_op jit(solution)/shard_map/ppermute | solution.py:31
  256.0 3.0 %hand_over.7 = bf16[4,320,384]{2,1,0:T(8,128)(2,1)} custom-call(s32[1]{0:T(128)} %bitcast.19.start_ref, bf16[320,640]{1,0:T(8,128)(2,1)S(1)} %fusion.1.refs_0_.refs_8_, bf16[320,640]{1,0:T(8,128)(2,1)} %collective-permute-done.26.refs_1_.refs_9_, bf16[320,640]{1,0:T(8,128)(2,1)} %collective-permute-done.27.refs_2_.refs_10_, ...), custom_call_target="tpu_custom_call" | custom-call | bytes 1966080 | tf_op jit(solution)/shard_map/hand_over/pallas_call | solution.py:297
  262.5 2.9 %collective-permute-done.44.refs_3_.refs_20_ = bf16[80,640]{1,0:T(8,128)(2,1)S(1)} collective-permute-done((bf16[80,640]{1,0:T(8,128)(2,1)S(1)}, bf16[80,640]{1,0:T(8,128)(2,1)S(1)}, u32[]{:S(2)}, u32[]{:S(2)}) %collective-permute-start.44) | collective-permute-done | bytes 102432 | tf_op jit(solution)/shard_map/ppermute | solution.py:31
  269.2 4.2 %collective-permute-done.7.refs_1_ = bf16[160,640]{1,0:T(8,128)(2,1)S(1)} collective-permute-done((bf16[160,640]{1,0:T(8,128)(2,1)S(1)}, bf16[160,640]{1,0:T(8,128)(2,1)S(1)}, u32[]{:S(2)}, u32[]{:S(2)}) %collective-permute-start.7) | collective-permute-done | bytes 204832 | tf_op jit(solution)/shard_map/ppermute | solution.py:31
  273.4 3.0 %collective-permute-done.9.refs_3_ = bf16[160,640]{1,0:T(8,128)(2,1)S(1)} collective-permute-done((bf16[160,640]{1,0:T(8,128)(2,1)}, bf16[160,640]{1,0:T(8,128)(2,1)S(1)}, u32[]{:S(2)}, u32[]{:S(2)}) %collective-permute-start.9) | collective-permute-done | bytes 204832 | tf_op jit(solution)/shard_map/ppermute | solution.py:31
  281.8 9.1 %mix.1 = f32[2,320,2560]{2,1,0:T(8,128)} custom-call(s32[6]{0:T(128)} %stack.46.info_ref, f32[2,4]{1,0:T(2,128)} %w_ref.1, bf16[160,640]{1,0:T(8,128)(2,1)} %copy-done.9, bf16[160,640]{1,0:T(8,128)(2,1)} %copy-done.19, bf16[160,640]{1,0:T(8,128)(2,1)} %collective-permute-done.8.refs_2_, bf16[160,640]{1,0:T(8,128)(2,1)} %copy-done.20, ...), custom_call_target="tpu_custom_call" | custom-call | tf_op jit(solution)/shard_map/mix/pallas_call | solution.py:388
  (156 shorter events, 69.6 us)
Async XLA Ops:
  0.0 92.3 %collective-permute-start.3 = (bf16[512,4096]{1,0:T(8,128)(2,1)}, bf16[512,4096]{1,0:T(8,128)(2,1)}, u32[]{:S(2)}, u32[]{:S(2)}) collective-permute-start(bf16[512,4096]{1,0:T(8,128)(2,1)} %bitcast.40), channel_id=1, source_target_pairs={{0,1},{1,0},{2,3},{3,2},{4,5},{5,4},{6,7},{7,6},{8,9},{9,8},{10,11... | collective-permute-start | bytes 12582920 | tf_op jit(solution)/shard_map/ppermute | solution.py:31
  0.5 18.2 %collective-permute-start = (bf16[80,4096]{1,0:T(8,128)(2,1)}, bf16[80,4096]{1,0:T(8,128)(2,1)S(1)}, u32[]{:S(2)}, u32[]{:S(2)}) collective-permute-start(bf16[80,4096]{1,0:T(8,128)(2,1)} %refs_1_.1), channel_id=1, source_target_pairs={{0,2},{1,3},{2,0},{3,1},{4,6},{5,7},{6,4},{7,5},{8,10},{9,11},{10,... | collective-permute-start | bytes 1966088 | tf_op jit(solution)/shard_map/ppermute | solution.py:31
  3.1 18.8 %collective-permute-start.1 = (bf16[80,4096]{1,0:T(8,128)(2,1)}, bf16[80,4096]{1,0:T(8,128)(2,1)}, u32[]{:S(2)}, u32[]{:S(2)}) collective-permute-start(bf16[80,4096]{1,0:T(8,128)(2,1)} %refs_1_.1), channel_id=1, source_target_pairs={{0,0},{1,1},{2,4},{3,5},{4,2},{5,3},{6,6},{7,7},{8,8},{9,9},{10,12... | collective-permute-start | bytes 1966088 | tf_op jit(solution)/shard_map/ppermute | solution.py:31
  9.6 17.8 %collective-permute-start.20 = (bf16[80,4096]{1,0:T(8,128)(2,1)}, bf16[80,4096]{1,0:T(8,128)(2,1)S(1)}, u32[]{:S(2)}, u32[]{:S(2)}) collective-permute-start(bf16[80,4096]{1,0:T(8,128)(2,1)} %refs_1_.1), channel_id=1, source_target_pairs={{0,16},{1,17},{2,18},{3,19},{4,20},{5,21},{6,22},{7,23},{8,24},{9,... | collective-permute-start | bytes 1966088 | tf_op jit(solution)/shard_map/ppermute | solution.py:31
  18.7 22.0 %collective-permute-start.21 = (bf16[80,4096]{1,0:T(8,128)(2,1)S(1)}, bf16[80,4096]{1,0:T(8,128)(2,1)S(1)}, u32[]{:S(2)}, u32[]{:S(2)}) collective-permute-start(bf16[80,4096]{1,0:T(8,128)(2,1)S(1)} %collective-permute-done.refs_1_.refs_0_), channel_id=1, source_target_pairs={{0,16},{1,17},{2,18},{3,19},{4,20},{5,21},{6,22},{7,23},{8,24},{9,... | collective-permute-start | bytes 1966088 | tf_op jit(solution)/shard_map/ppermute | solution.py:31
  20.4 53.4 %collective-permute-start.12 = (bf16[80,4096]{1,0:T(8,128)(2,1)}, bf16[80,4096]{1,0:T(8,128)(2,1)S(1)}, u32[]{:S(2)}, u32[]{:S(2)}) collective-permute-start(bf16[80,4096]{1,0:T(8,128)(2,1)} %refs_1_.1), channel_id=1, source_target_pairs={{0,8},{1,9},{2,10},{3,11},{4,12},{5,13},{6,14},{7,15},{8,0},{9,1},... | collective-permute-start | bytes 1966088 | tf_op jit(solution)/shard_map/ppermute | solution.py:31
  21.9 78.3 %collective-permute-start.4 = (bf16[2560,512]{1,0:T(8,128)(2,1)}, bf16[2560,512]{1,0:T(8,128)(2,1)S(1)}, u32[]{:S(2)}, u32[]{:S(2)}) collective-permute-start(bf16[2560,512]{1,0:T(8,128)(2,1)} %own_ref.9), channel_id=1, source_target_pairs={{0,1},{1,0},{2,3},{3,2},{4,5},{5,4},{6,7},{7,6},{8,9},{9,8},{10,11... | collective-permute-start | bytes 7864328 | tf_op jit(solution)/shard_map/ppermute | solution.py:31
  27.5 30.9 %collective-permute-start.10 = (bf16[80,4096]{1,0:T(8,128)(2,1)S(1)}, bf16[80,4096]{1,0:T(8,128)(2,1)S(1)}, u32[]{:S(2)}, u32[]{:S(2)}) collective-permute-start(bf16[80,4096]{1,0:T(8,128)(2,1)S(1)} %collective-permute-done.refs_1_.refs_0_), channel_id=1, source_target_pairs={{0,0},{1,1},{2,4},{3,5},{4,2},{5,3},{6,6},{7,7},{8,8},{9,9},{10,12... | collective-permute-start | bytes 1966088 | tf_op jit(solution)/shard_map/ppermute | solution.py:31
  56.9 18.5 %collective-permute-start.13 = (bf16[80,4096]{1,0:T(8,128)(2,1)S(1)}, bf16[80,4096]{1,0:T(8,128)(2,1)S(1)}, u32[]{:S(2)}, u32[]{:S(2)}) collective-permute-start(bf16[80,4096]{1,0:T(8,128)(2,1)S(1)} %collective-permute-done.refs_1_.refs_0_), channel_id=1, source_target_pairs={{0,8},{1,9},{2,10},{3,11},{4,12},{5,13},{6,14},{7,15},{8,0},{9,1},... | collective-permute-start | bytes 1966088 | tf_op jit(solution)/shard_map/ppermute | solution.py:31
  73.8 41.3 %collective-permute-start.30 = (bf16[80,4096]{1,0:T(8,128)(2,1)S(1)}, bf16[80,4096]{1,0:T(8,128)(2,1)S(1)}, u32[]{:S(2)}, u32[]{:S(2)}) collective-permute-start(bf16[80,4096]{1,0:T(8,128)(2,1)S(1)} %get-tuple-element.26), channel_id=1, source_target_pairs={{0,8},{1,9},{2,10},{3,11},{4,12},{5,13},{6,14},{7,15},{8,0},{9,1},... | collective-permute-start | bytes 1966088 | tf_op jit(solution)/shard_map/ppermute | solution.py:31
  75.3 43.5 %collective-permute-start.23 = (bf16[80,4096]{1,0:T(8,128)(2,1)S(1)}, bf16[80,4096]{1,0:T(8,128)(2,1)S(1)}, u32[]{:S(2)}, u32[]{:S(2)}) collective-permute-start(bf16[80,4096]{1,0:T(8,128)(2,1)S(1)} %broadcast_select_fusion.2.refs_2_), channel_id=1, source_target_pairs={{0,8},{1,9},{2,10},{3,11},{4,12},{5,13},{6,14},{7,15},{8,0},{9,1},... | collective-permute-start | bytes 1966088 | tf_op jit(solution)/shard_map/ppermute | solution.py:31
  90.8 29.6 %collective-permute-start.29 = (bf16[80,4096]{1,0:T(8,128)(2,1)S(1)}, bf16[80,4096]{1,0:T(8,128)(2,1)S(1)}, u32[]{:S(2)}, u32[]{:S(2)}) collective-permute-start(bf16[80,4096]{1,0:T(8,128)(2,1)S(1)} %broadcast_select_fusion.2.refs_2_), channel_id=1, source_target_pairs={{0,16},{1,17},{2,18},{3,19},{4,20},{5,21},{6,22},{7,23},{8,24},{9,... | collective-permute-start | bytes 1966088 | tf_op jit(solution)/shard_map/ppermute | solution.py:31
  92.3 30.1 %collective-permute-start.31 = (bf16[80,4096]{1,0:T(8,128)(2,1)S(1)}, bf16[80,4096]{1,0:T(8,128)(2,1)S(1)}, u32[]{:S(2)}, u32[]{:S(2)}) collective-permute-start(bf16[80,4096]{1,0:T(8,128)(2,1)S(1)} %collective-permute-done.14.refs_5_), channel_id=1, source_target_pairs={{0,16},{1,17},{2,18},{3,19},{4,20},{5,21},{6,22},{7,23},{8,24},{9,... | collective-permute-start | bytes 1966088 | tf_op jit(solution)/shard_map/ppermute | solution.py:31
  100.3 35.1 %collective-permute-start.22 = (bf16[80,4096]{1,0:T(8,128)(2,1)S(1)}, bf16[80,4096]{1,0:T(8,128)(2,1)S(1)}, u32[]{:S(2)}, u32[]{:S(2)}) collective-permute-start(bf16[80,4096]{1,0:T(8,128)(2,1)S(1)} %broadcast_select_fusion.3.refs_2_), channel_id=1, source_target_pairs={{0,16},{1,17},{2,18},{3,19},{4,20},{5,21},{6,22},{7,23},{8,24},{9,... | collective-permute-start | bytes 1966088 | tf_op jit(solution)/shard_map/ppermute | solution.py:31
  115.1 32.3 %collective-permute-start.38 = (bf16[80,4096]{1,0:T(8,128)(2,1)S(1)}, bf16[80,4096]{1,0:T(8,128)(2,1)S(1)}, u32[]{:S(2)}, u32[]{:S(2)}) collective-permute-start(bf16[80,4096]{1,0:T(8,128)(2,1)S(1)} %get-tuple-element.25), channel_id=1, source_target_pairs={{0,8},{1,9},{2,10},{3,11},{4,12},{5,13},{6,14},{7,15},{8,0},{9,1},... | collective-permute-start | bytes 1966088 | tf_op jit(solution)/shard_map/ppermute | solution.py:31
  118.9 29.5 %collective-permute-start.39 = (bf16[80,4096]{1,0:T(8,128)(2,1)S(1)}, bf16[80,4096]{1,0:T(8,128)(2,1)S(1)}, u32[]{:S(2)}, u32[]{:S(2)}) collective-permute-start(bf16[80,4096]{1,0:T(8,128)(2,1)S(1)} %collective-permute-done.23.refs_5_), channel_id=1, source_target_pairs={{0,16},{1,17},{2,18},{3,19},{4,20},{5,21},{6,22},{7,23},{8,24},{9,... | collective-permute-start | bytes 1966088 | tf_op jit(solution)/shard_map/ppermute | solution.py:31
  120.4 39.0 %collective-permute-start.5 = (bf16[2,160,640]{2,1,0:T(8,128)(2,1)S(1)}, bf16[2,160,640]{2,1,0:T(8,128)(2,1)S(1)}, u32[]{:S(2)}, u32[]{:S(2)}) collective-permute-start(bf16[2,160,640]{2,1,0:T(8,128)(2,1)S(1)} %get-tuple-element.16), channel_id=1, source_target_pairs={{0,2},{1,3},{2,0},{3,1},{4,6},{5,7},{6,4},{7,5},{8,10},{9,11},{10,... | collective-permute-start | bytes 1228808 | tf_op jit(solution)/shard_map/ppermute | solution.py:31
  122.4 37.0 %collective-permute-start.15 = (bf16[2,320,640]{2,1,0:T(8,128)(2,1)S(1)}, bf16[2,320,640]{2,1,0:T(8,128)(2,1)S(1)}, u32[]{:S(2)}, u32[]{:S(2)}) collective-permute-start(bf16[2,320,640]{2,1,0:T(8,128)(2,1)S(1)} %get-tuple-element.18), channel_id=1, source_target_pairs={{0,2},{1,3},{2,0},{3,1},{4,6},{5,7},{6,4},{7,5},{8,10},{9,11},{10,... | collective-permute-start | bytes 2457608 | tf_op jit(solution)/shard_map/ppermute | solution.py:31
  135.3 32.5 %collective-permute-start.32 = (bf16[2,320,640]{2,1,0:T(8,128)(2,1)S(1)}, bf16[2,320,640]{2,1,0:T(8,128)(2,1)S(1)}, u32[]{:S(2)}, u32[]{:S(2)}) collective-permute-start(bf16[2,320,640]{2,1,0:T(8,128)(2,1)S(1)} %get-tuple-element.22), channel_id=1, source_target_pairs={{0,2},{1,3},{2,0},{3,1},{4,6},{5,7},{6,4},{7,5},{8,10},{9,11},{10,... | collective-permute-start | bytes 2457608 | tf_op jit(solution)/shard_map/ppermute | solution.py:31
  147.4 36.1 %collective-permute-start.24 = (bf16[2,320,640]{2,1,0:T(8,128)(2,1)S(1)}, bf16[2,320,640]{2,1,0:T(8,128)(2,1)S(1)}, u32[]{:S(2)}, u32[]{:S(2)}) collective-permute-start(bf16[2,320,640]{2,1,0:T(8,128)(2,1)S(1)} %get-tuple-element.20), channel_id=1, source_target_pairs={{0,2},{1,3},{2,0},{3,1},{4,6},{5,7},{6,4},{7,5},{8,10},{9,11},{10,... | collective-permute-start | bytes 2457608 | tf_op jit(solution)/shard_map/ppermute | solution.py:31
  158.2 57.7 %collective-permute-start.40 = (bf16[2,160,640]{2,1,0:T(8,128)(2,1)S(1)}, bf16[2,160,640]{2,1,0:T(8,128)(2,1)S(1)}, u32[]{:S(2)}, u32[]{:S(2)}) collective-permute-start(bf16[2,160,640]{2,1,0:T(8,128)(2,1)S(1)} %get-tuple-element.24), channel_id=1, source_target_pairs={{0,2},{1,3},{2,0},{3,1},{4,6},{5,7},{6,4},{7,5},{8,10},{9,11},{10,... | collective-permute-start | bytes 1228808 | tf_op jit(solution)/shard_map/ppermute | solution.py:31
  159.6 44.5 %collective-permute-start.16 = (bf16[320,640]{1,0:T(8,128)(2,1)S(1)}, bf16[320,640]{1,0:T(8,128)(2,1)S(1)}, u32[]{:S(2)}, u32[]{:S(2)}) collective-permute-start(bf16[320,640]{1,0:T(8,128)(2,1)S(1)} %fusion.3), channel_id=1, source_target_pairs={{0,6},{1,7},{2,4},{3,5},{4,2},{5,3},{6,0},{7,1},{8,14},{9,15},{10,... | collective-permute-start | bytes 1228808 | tf_op jit(solution)/shard_map/ppermute | solution.py:31
  167.9 41.4 %collective-permute-start.33 = (bf16[320,640]{1,0:T(8,128)(2,1)S(1)}, bf16[320,640]{1,0:T(8,128)(2,1)S(1)}, u32[]{:S(2)}, u32[]{:S(2)}) collective-permute-start(bf16[320,640]{1,0:T(8,128)(2,1)S(1)} %fusion.5), channel_id=1, source_target_pairs={{0,6},{1,7},{2,4},{3,5},{4,2},{5,3},{6,0},{7,1},{8,14},{9,15},{10,... | collective-permute-start | bytes 1228808 | tf_op jit(solution)/shard_map/ppermute | solution.py:31
  183.6 31.7 %collective-permute-start.25 = (bf16[320,640]{1,0:T(8,128)(2,1)S(1)}, bf16[320,640]{1,0:T(8,128)(2,1)S(1)}, u32[]{:S(2)}, u32[]{:S(2)}) collective-permute-start(bf16[320,640]{1,0:T(8,128)(2,1)S(1)} %fusion.4), channel_id=1, source_target_pairs={{0,6},{1,7},{2,4},{3,5},{4,2},{5,3},{6,0},{7,1},{8,14},{9,15},{10,... | collective-permute-start | bytes 1228808 | tf_op jit(solution)/shard_map/ppermute | solution.py:31
  204.2 29.9 %collective-permute-start.17 = (bf16[320,640]{1,0:T(8,128)(2,1)S(1)}, bf16[320,640]{1,0:T(8,128)(2,1)S(1)}, u32[]{:S(2)}, u32[]{:S(2)}) collective-permute-start(bf16[320,640]{1,0:T(8,128)(2,1)S(1)} %fusion.2.refs_0_.refs_4_), channel_id=1, source_target_pairs={{0,8},{1,9},{2,10},{3,11},{4,12},{5,13},{6,14},{7,15},{8,0},{9,1},... | collective-permute-start | bytes 1228808 | tf_op jit(solution)/shard_map/ppermute | solution.py:31
  204.8 29.9 %collective-permute-start.18 = (bf16[320,640]{1,0:T(8,128)(2,1)S(1)}, bf16[320,640]{1,0:T(8,128)(2,1)S(1)}, u32[]{:S(2)}, u32[]{:S(2)}) collective-permute-start(bf16[320,640]{1,0:T(8,128)(2,1)S(1)} %fusion.2.refs_0_.refs_4_), channel_id=1, source_target_pairs={{0,16},{1,17},{2,18},{3,19},{4,20},{5,21},{6,22},{7,23},{8,24},{9,... | collective-permute-start | bytes 1228808 | tf_op jit(solution)/shard_map/ppermute | solution.py:31
  215.9 20.3 %collective-permute-start.27 = (bf16[320,640]{1,0:T(8,128)(2,1)S(1)}, bf16[320,640]{1,0:T(8,128)(2,1)}, u32[]{:S(2)}, u32[]{:S(2)}) collective-permute-start(bf16[320,640]{1,0:T(8,128)(2,1)S(1)} %fusion.1.refs_0_.refs_8_), channel_id=1, source_target_pairs={{0,16},{1,17},{2,18},{3,19},{4,20},{5,21},{6,22},{7,23},{8,24},{9,... | collective-permute-start | bytes 1228808 | tf_op jit(solution)/shard_map/ppermute | solution.py:31
  227.4 28.1 %collective-permute-start.26 = (bf16[320,640]{1,0:T(8,128)(2,1)S(1)}, bf16[320,640]{1,0:T(8,128)(2,1)}, u32[]{:S(2)}, u32[]{:S(2)}) collective-permute-start(bf16[320,640]{1,0:T(8,128)(2,1)S(1)} %fusion.1.refs_0_.refs_8_), channel_id=1, source_target_pairs={{0,8},{1,9},{2,10},{3,11},{4,12},{5,13},{6,14},{7,15},{8,0},{9,1},... | collective-permute-start | bytes 1228808 | tf_op jit(solution)/shard_map/ppermute | solution.py:31
  236.2 19.2 %collective-permute-start.28 = (bf16[320,640]{1,0:T(8,128)(2,1)}, bf16[320,640]{1,0:T(8,128)(2,1)}, u32[]{:S(2)}, u32[]{:S(2)}) collective-permute-start(bf16[320,640]{1,0:T(8,128)(2,1)} %collective-permute-done.27.refs_2_.refs_10_), channel_id=1, source_target_pairs={{0,8},{1,9},{2,10},{3,11},{4,12},{5,13},{6,14},{7,15},{8,0},{9,1},... | collective-permute-start | bytes 1228808 | tf_op jit(solution)/shard_map/ppermute | solution.py:31
  255.4 24.7 %collective-permute-start.49 = (bf16[4,320,384]{2,1,0:T(8,128)(2,1)}, bf16[4,320,384]{2,1,0:T(8,128)(2,1)}, u32[]{:S(2)}, u32[]{:S(2)}) collective-permute-start(bf16[4,320,384]{2,1,0:T(8,128)(2,1)} %hand_over.8), channel_id=1, source_target_pairs={{0,1},{1,0},{2,3},{3,2},{4,5},{5,4},{6,7},{7,6},{8,9},{9,8},{10,11... | collective-permute-start | bytes 2949128 | tf_op jit(solution)/shard_map/ppermute | solution.py:31
  255.5 24.6 %collective-permute-start.47 = (bf16[4,320,384]{2,1,0:T(8,128)(2,1)}, bf16[4,320,384]{2,1,0:T(8,128)(2,1)}, u32[]{:S(2)}, u32[]{:S(2)}) collective-permute-start(bf16[4,320,384]{2,1,0:T(8,128)(2,1)} %hand_over.6), channel_id=1, source_target_pairs={{0,1},{1,0},{2,3},{3,2},{4,5},{5,4},{6,7},{7,6},{8,9},{9,8},{10,11... | collective-permute-start | bytes 2949128 | tf_op jit(solution)/shard_map/ppermute | solution.py:31
  259.0 21.1 %collective-permute-start.48 = (bf16[4,320,384]{2,1,0:T(8,128)(2,1)}, bf16[4,320,384]{2,1,0:T(8,128)(2,1)S(1)}, u32[]{:S(2)}, u32[]{:S(2)}) collective-permute-start(bf16[4,320,384]{2,1,0:T(8,128)(2,1)} %hand_over.7), channel_id=1, source_target_pairs={{0,1},{1,0},{2,3},{3,2},{4,5},{5,4},{6,7},{7,6},{8,9},{9,8},{10,11... | collective-permute-start | bytes 2949128 | tf_op jit(solution)/shard_map/ppermute | solution.py:31
  (44 other events, 760.1 us)

commit v3 on v2

--- a/solution.py
+++ b/solution.py
@@ -262,8 +262,8 @@
             grid=(steps,),
             in_specs=[
                 pl.BlockSpec((c, depth), lambda i, o: (0, 0)),
-                pl.BlockSpec((chip_rows, half), lambda i, o: (o[i], 0)),
-                pl.BlockSpec((chip_rows, half), lambda i, o: (o[i], 0)),
+                pl.BlockSpec((chip_rows, half), lambda i, o: (o[2 + i], 0)),
+                pl.BlockSpec((chip_rows, half), lambda i, o: (o[2 + i], 0)),
             ],
             out_specs=[
                 pl.BlockSpec((1, c, chip_rows), lambda i, o: (jnp.minimum(i, 1), 0, 0)),
@@ -299,7 +299,7 @@
         grid_spec=pltpu.PrefetchScalarGridSpec(
             num_scalar_prefetch=1,
             grid=(width,),
-            in_specs=[pl.BlockSpec((n, LANES), lambda i, s: (0, s[0] + i)) for n in counts],
+            in_specs=[pl.BlockSpec((n, LANES), lambda i, s: (0, s[12] + i)) for n in counts],
             out_specs=pl.BlockSpec((sources, c, LANES), lambda i, s: (0, 0, i)),
         ),
         out_shape=jax.ShapeDtypeStruct((sources, c, window), parts[0].dtype),
@@ -326,7 +326,7 @@
         got = refs[total : total + pieces]
         out_ref, own, other, acc, turned, sems = refs[total + pieces :]
         step = pl.program_id(0)
-        me, core = info_ref[0], info_ref[1]
+        me, core = info_ref[6], info_ref[7]
         lane = pl.multiple_of(core * first, LANES)
 
         def copies(ring):
@@ -366,7 +366,7 @@
                     copy.wait()
 
         for s in range(slots):
-            z = info_ref[2 + s]
+            z = info_ref[8 + s]
             for which in range(2):
                 held_at = own if which == 0 else other
                 base = z * unit + (core if which == 0 else 1 - core) * held
@@ -391,7 +391,7 @@
             num_scalar_prefetch=2,
             grid=(rels,),
             in_specs=[pl.BlockSpec(memory_space=pl.ANY)] * (len(flat_parts) + pieces),
-            out_specs=pl.BlockSpec((targets, own_rows, tall), lambda i, a, b: (0, 0, i ^ a[0])),
+            out_specs=pl.BlockSpec((targets, own_rows, tall), lambda i, a, b: (0, 0, i ^ a[6])),
             scratch_shapes=[
                 pltpu.VMEM((rels, sources, slots * held, window), jnp.bfloat16),
                 pltpu.VMEM((rels, sources, slots * held, window), jnp.bfloat16),
@@ -456,14 +456,14 @@
 
     flip = lambda m: jnp.where(right, chips - 1 - m, m)
     ints = lambda *v: jnp.stack([jnp.asarray(x, jnp.int32) for x in v])
-    order = ints(*[flip(jnp.where(inner, m, e)) for m, e in ((0, 1), (3, 2), (1, 0), (2, 3))])
-    place = ints(inner, right)
+    blocks = [flip(jnp.where(inner, m, e)) for m, e in ((0, 1), (3, 2), (1, 0), (2, 3))]
+    table = ints(inner, right, *blocks, me, core, 1, 2, 0, 3, jnp.where(core == 0, first // LANES, 0))
     f32 = jnp.float32
 
     kept, given = [], []
     for i, piece in enumerate(PIECES):
-        near = project([unit(*u) for u in piece], h, place, mine, theirs)
-        give, keep = expand(order, near, outs, chip_rows)
+        near = project([unit(*u) for u in piece], h, table, mine, theirs)
+        give, keep = expand(table, near, outs, chip_rows)
         got = pair(give)
         last = mirror((keep[1].astype(f32) + got[1].astype(f32)).astype(jnp.bfloat16))
         expanded = (keep[0].astype(f32) + got[0].astype(f32) + last.astype(f32)).astype(jnp.bfloat16)
@@ -474,13 +474,11 @@
             cut = expanded.shape[0] // 2
             diagonal = [over_x(from_y[:cut]), over_y(from_x[cut:])]
         spread = [expanded, from_x, from_y, *diagonal]
-        start = ints(jnp.where(core == 0, first // LANES, 0))
-        give = hand_over(start, spread, [part.shape[0] for part in spread], window)
+        give = hand_over(table, spread, [part.shape[0] for part in spread], window)
         kept.append(spread)
         given.append(partner(give))
 
-    info = ints(me, core, 1, 2, 0, 3)
-    return mix(info, depth, kept, given, own_rows, window, first, h, columns)
+    return mix(table, depth, kept, given, own_rows, window, first, h, columns)
 
 
 def on_device(source, expand_out, expand_in, depth):

time: 292 us -> 292 us (level)
  the two profiles are of different devices: /device:TPU:0 before, /device:TPU:11 now
where the time goes in v3:
time: 292 us; the launch traced here: 291 us
  waiting for transfers between devices  135 us (46%)
  starting transfers between devices  72.1 us (25%)
  Pallas kernels  69.5 us (24%)
  local copies, waits for them, and re-layouts  8.4 us (3%)
  other arithmetic  5.37 us (2%)
    ppermute x51, waiting for transfers between devices, send(): return lax.ppermute(value, AXES, pairs)  135 us
    ppermute x51, starting transfers between devices, send(): return lax.ppermute(value, AXES, pairs)  72.1 us
    pallas_call x5, Pallas kernels, project(): pl.pallas_call(kernel, grid_spec=pltpu.PrefetchScalarGridSpec(num_scalar_...  38.4 us
    pallas_call x5, Pallas kernels, expand(): pl.pallas_call(kernel, grid_spec=pltpu.PrefetchScalarGridSpec(num_scalar_...  16.6 us
    pallas_call x1, Pallas kernels, mix(): pl.pallas_call(kernel, grid_spec=pltpu.PrefetchScalarGridSpec(num_scalar_...  9.14 us
    unnamed x76, local copies, waits for them, and re-layouts  8.26 us
  transfers between devices with their start and end apart: 51, of which 20 were waited for; matrix products, arithmetic and copies ran while one was open for 2% of the time, Pallas kernels for 21%

profile of v3, /device:TPU:11, one launch (start us, length us, event | category | flops | bytes accessed | tf_op | source)
XLA Modules:
  0.0 290.7 jit_solution(704752709330194301)
XLA Ops:
  0.8 4.3 %collective-permute-start.1 = (bf16[80,4096]{1,0:T(8,128)(2,1)}, bf16[80,4096]{1,0:T(8,128)(2,1)}, u32[]{:S(2)}, u32[]{:S(2)}) collective-permute-start(bf16[80,4096]{1,0:T(8,128)(2,1)} %refs_1_.1), channel_id=1, source_target_pairs={{0,0},{1,1},{2,4},{3,5},{4,2},{5,3},{6,6},{7,7},{8,8},{9,9},{10,12... | collective-permute-start | bytes 1966088 | tf_op jit(solution)/shard_map/ppermute | solution.py:31
  6.5 10.8 %collective-permute-done.refs_1_.refs_0_ = bf16[80,4096]{1,0:T(8,128)(2,1)} collective-permute-done((bf16[80,4096]{1,0:T(8,128)(2,1)}, bf16[80,4096]{1,0:T(8,128)(2,1)}, u32[]{:S(2)}, u32[]{:S(2)}) %collective-permute-start) | collective-permute-done | bytes 655392 | tf_op jit(solution)/shard_map/ppermute | solution.py:31
  21.2 3.3 %collective-permute-start.10 = (bf16[80,4096]{1,0:T(8,128)(2,1)}, bf16[80,4096]{1,0:T(8,128)(2,1)S(1)}, u32[]{:S(2)}, u32[]{:S(2)}) collective-permute-start(bf16[80,4096]{1,0:T(8,128)(2,1)} %collective-permute-done.refs_1_.refs_0_), channel_id=1, source_target_pairs={{0,0},{1,1},{2,4},{3,5},{4,2},{5,3},{6,6},{7,7},{8,8},{9,9},{10,12... | collective-permute-start | bytes 1966088 | tf_op jit(solution)/shard_map/ppermute | solution.py:31
  24.5 10.8 %collective-permute-done.21.refs_1_.refs_0_ = bf16[80,4096]{1,0:T(8,128)(2,1)} collective-permute-done((bf16[80,4096]{1,0:T(8,128)(2,1)}, bf16[80,4096]{1,0:T(8,128)(2,1)}, u32[]{:S(2)}, u32[]{:S(2)}) %collective-permute-start.21) | collective-permute-done | bytes 655392 | tf_op jit(solution)/shard_map/ppermute | solution.py:31
  35.3 3.7 %collective-permute-start.2 = (bf16[80,4096]{1,0:T(8,128)(2,1)}, bf16[80,4096]{1,0:T(8,128)(2,1)S(1)}, u32[]{:S(2)}, u32[]{:S(2)}) collective-permute-start(bf16[80,4096]{1,0:T(8,128)(2,1)} %collective-permute-done.1), channel_id=1, source_target_pairs={{0,2},{1,3},{2,0},{3,1},{4,6},{5,7},{6,4},{7,5},{8,10},{9,11},{10,... | collective-permute-start | bytes 1966088 | tf_op jit(solution)/shard_map/ppermute | solution.py:31
  39.1 2.3 broadcast_select_fusion
  41.3 11.9 %collective-permute-done.2 = bf16[80,4096]{1,0:T(8,128)(2,1)S(1)} collective-permute-done((bf16[80,4096]{1,0:T(8,128)(2,1)}, bf16[80,4096]{1,0:T(8,128)(2,1)S(1)}, u32[]{:S(2)}, u32[]{:S(2)}) %collective-permute-start.2) | collective-permute-done | bytes 655392 | tf_op jit(solution)/shard_map/ppermute | solution.py:31
  57.1 10.7 %collective-permute-done.11 = bf16[80,4096]{1,0:T(8,128)(2,1)S(1)} collective-permute-done((bf16[80,4096]{1,0:T(8,128)(2,1)S(1)}, bf16[80,4096]{1,0:T(8,128)(2,1)S(1)}, u32[]{:S(2)}, u32[]{:S(2)}) %collective-permute-start.11) | collective-permute-done | bytes 655392 | tf_op jit(solution)/shard_map/ppermute | solution.py:31
  71.1 11.1 %collective-permute-done.14.refs_5_ = bf16[80,4096]{1,0:T(8,128)(2,1)} collective-permute-done((bf16[80,4096]{1,0:T(8,128)(2,1)S(1)}, bf16[80,4096]{1,0:T(8,128)(2,1)}, u32[]{:S(2)}, u32[]{:S(2)}) %collective-permute-start.14) | collective-permute-done | bytes 655392 | tf_op jit(solution)/shard_map/ppermute | solution.py:31
  83.7 2.2 copy-done
  88.1 8.4 %project.6.near_ref = bf16[320,1024]{1,0:T(8,128)(2,1)S(1)} custom-call(s32[13]{0:T(128)S(1)} %stack.47.inner_ref.order_ref.start_ref.info_ref, bf16[80,4096]{1,0:T(8,128)(2,1)} %collective-permute-done.refs_1_.refs_0_, bf16[80,4096]{1,0:T(8,128)(2,1)S(1)} %copy-done.9, bf16[80,4096]{1,0:T(8,128)(2,1)} %broadcast_select_fusion.2.refs_2_, ...), custom_call_target="tpu_custom_call" | custom-call | flops 2684354560 | bytes 11665408 | tf_op jit(solution)/shard_map/project/pallas_call | solution.py:215
  97.9 6.8 %project.5.near_ref = bf16[160,1024]{1,0:T(8,128)(2,1)S(1)} custom-call(s32[13]{0:T(128)S(1)} %stack.47.inner_ref.order_ref.start_ref.info_ref, bf16[80,4096]{1,0:T(8,128)(2,1)S(1)} %copy-done.9, bf16[80,4096]{1,0:T(8,128)(2,1)} %collective-permute-done.refs_1_.refs_0_, bf16[80,4096]{1,0:T(8,128)(2,1)S(1)} %copy-done.11, bf16[512,4096]{1,0:T(8,128)(2,1)S(1)} %bitcast.42, ...), custom_call_target="tpu_custom_call" | custom-call | flops 1342177280 | bytes 10027008 | tf_op jit(solution)/shard_map/project/pallas_call | solution.py:215
  104.7 2.9 expand.5
  107.6 3.6 %expand.6 = (bf16[2,320,640]{2,1,0:T(8,128)(2,1)S(1)}, bf16[2,320,640]{2,1,0:T(8,128)(2,1)S(1)}) custom-call(s32[13]{0:T(128)S(1)} %stack.47.inner_ref.order_ref.start_ref.info_ref, bf16[320,1024]{1,0:T(8,128)(2,1)S(1)} %project.6.near_ref, bf16[2560,512]{1,0:T(8,128)(2,1)S(1)} %copy-done.2, bf16[2560,512]{1,0:T(8,128)(2,1)S(1)} %collective-permute-done.4.far_ref), custom_call_target="tpu_custom_call" | custom-call | flops 1677721600 | bytes 7536640 | tf_op jit(solution)/shard_map/expand/pallas_call | solution.py:258
  113.2 8.2 %project.8.near_ref = bf16[320,1024]{1,0:T(8,128)(2,1)S(1)} custom-call(s32[13]{0:T(128)S(1)} %stack.47.inner_ref.order_ref.start_ref.info_ref, bf16[80,4096]{1,0:T(8,128)(2,1)} %collective-permute-done.21.refs_1_.refs_0_, bf16[80,4096]{1,0:T(8,128)(2,1)S(1)} %collective-permute-done.20.refs_0_.refs_1_, bf16[80,4096]{1,0:T(8,128)(2,1)} %collective-permute-done.29.refs_2_, ...), custom_call_target="tpu_custom_call" | custom-call | flops 2684354560 | bytes 11665408 | tf_op jit(solution)/shard_map/project/pallas_call | solution.py:215
  121.4 3.6 %expand.8 = (bf16[2,320,640]{2,1,0:T(8,128)(2,1)S(1)}, bf16[2,320,640]{2,1,0:T(8,128)(2,1)S(1)}) custom-call(s32[13]{0:T(128)S(1)} %stack.47.inner_ref.order_ref.start_ref.info_ref, bf16[320,1024]{1,0:T(8,128)(2,1)S(1)} %project.8.near_ref, bf16[2560,512]{1,0:T(8,128)(2,1)S(1)} %copy-done.2, bf16[2560,512]{1,0:T(8,128)(2,1)S(1)} %collective-permute-done.4.far_ref), custom_call_target="tpu_custom_call" | custom-call | flops 1677721600 | bytes 7536640 | tf_op jit(solution)/shard_map/expand/pallas_call | solution.py:258
  126.5 8.2 %project.7.near_ref = bf16[320,1024]{1,0:T(8,128)(2,1)S(1)} custom-call(s32[13]{0:T(128)S(1)} %stack.47.inner_ref.order_ref.start_ref.info_ref, bf16[80,4096]{1,0:T(8,128)(2,1)S(1)} %collective-permute-done.20.refs_0_.refs_1_, bf16[80,4096]{1,0:T(8,128)(2,1)} %collective-permute-done.21.refs_1_.refs_0_, ...), custom_call_target="tpu_custom_call" | custom-call | flops 2684354560 | bytes 11665408 | tf_op jit(solution)/shard_map/project/pallas_call | solution.py:215
  134.7 3.6 %expand.7 = (bf16[2,320,640]{2,1,0:T(8,128)(2,1)S(1)}, bf16[2,320,640]{2,1,0:T(8,128)(2,1)S(1)}) custom-call(s32[13]{0:T(128)S(1)} %stack.47.inner_ref.order_ref.start_ref.info_ref, bf16[320,1024]{1,0:T(8,128)(2,1)S(1)} %project.7.near_ref, bf16[2560,512]{1,0:T(8,128)(2,1)S(1)} %copy-done.2, bf16[2560,512]{1,0:T(8,128)(2,1)S(1)} %collective-permute-done.4.far_ref), custom_call_target="tpu_custom_call" | custom-call | flops 1677721600 | bytes 7536640 | tf_op jit(solution)/shard_map/expand/pallas_call | solution.py:258
  138.4 6.8 %project.9.near_ref = bf16[160,1024]{1,0:T(8,128)(2,1)S(1)} custom-call(s32[13]{0:T(128)S(1)} %stack.47.inner_ref.order_ref.start_ref.info_ref, bf16[80,4096]{1,0:T(8,128)(2,1)S(1)} %collective-permute-done.38.refs_0_.refs_1_, bf16[80,4096]{1,0:T(8,128)(2,1)S(1)} %collective-permute-done.38.refs_0_.refs_1_, ...), custom_call_target="tpu_custom_call" | custom-call | flops 1342177280 | bytes 10027008 | tf_op jit(solution)/shard_map/project/pallas_call | solution.py:215
  145.2 3.0 %expand.9 = (bf16[2,160,640]{2,1,0:T(8,128)(2,1)S(1)}, bf16[2,160,640]{2,1,0:T(8,128)(2,1)S(1)}) custom-call(s32[13]{0:T(128)S(1)} %stack.47.inner_ref.order_ref.start_ref.info_ref, bf16[160,1024]{1,0:T(8,128)(2,1)S(1)} %project.9.near_ref, bf16[2560,512]{1,0:T(8,128)(2,1)S(1)} %copy-done.2, bf16[2560,512]{1,0:T(8,128)(2,1)S(1)} %collective-permute-done.4.far_ref), custom_call_target="tpu_custom_call" | custom-call | flops 838860800 | bytes 6389760 | tf_op jit(solution)/shard_map/expand/pallas_call | solution.py:258
  152.9 16.1 %collective-permute-done.24 = bf16[2,320,640]{2,1,0:T(8,128)(2,1)S(1)} collective-permute-done((bf16[2,320,640]{2,1,0:T(8,128)(2,1)S(1)}, bf16[2,320,640]{2,1,0:T(8,128)(2,1)S(1)}, u32[]{:S(2)}, u32[]{:S(2)}) %collective-permute-start.24) | collective-permute-done | bytes 819232 | tf_op jit(solution)/shard_map/ppermute | solution.py:31
  173.6 4.1 %collective-permute-done.25 = bf16[320,640]{1,0:T(8,128)(2,1)S(1)} collective-permute-done((bf16[320,640]{1,0:T(8,128)(2,1)S(1)}, bf16[320,640]{1,0:T(8,128)(2,1)S(1)}, u32[]{:S(2)}, u32[]{:S(2)}) %collective-permute-start.25) | collective-permute-done | bytes 409632 | tf_op jit(solution)/shard_map/ppermute | solution.py:31
  179.5 2.7 collective-permute-done.34.refs_1_.refs_13_
  182.4 2.4 collective-permute-done.35.refs_2_.refs_14_
  186.2 5.9 %collective-permute-done.6 = bf16[160,640]{1,0:T(8,128)(2,1)S(1)} collective-permute-done((bf16[160,640]{1,0:T(8,128)(2,1)S(1)}, bf16[160,640]{1,0:T(8,128)(2,1)S(1)}, u32[]{:S(2)}, u32[]{:S(2)}) %collective-permute-start.6) | collective-permute-done | bytes 204832 | tf_op jit(solution)/shard_map/ppermute | solution.py:31
  193.3 25.1 %collective-permute-done.41 = bf16[160,640]{1,0:T(8,128)(2,1)S(1)} collective-permute-done((bf16[160,640]{1,0:T(8,128)(2,1)S(1)}, bf16[160,640]{1,0:T(8,128)(2,1)S(1)}, u32[]{:S(2)}, u32[]{:S(2)}) %collective-permute-start.41) | collective-permute-done | bytes 204832 | tf_op jit(solution)/shard_map/ppermute | solution.py:31
  227.5 7.5 %collective-permute-done.19.refs_3_.refs_7_ = bf16[320,640]{1,0:T(8,128)(2,1)S(1)} collective-permute-done((bf16[320,640]{1,0:T(8,128)(2,1)S(1)}, bf16[320,640]{1,0:T(8,128)(2,1)S(1)}, u32[]{:S(2)}, u32[]{:S(2)}) %collective-permute-start.19) | collective-permute-done | bytes 409632 | tf_op jit(solution)/shard_map/ppermute | solution.py:31
  238.6 19.0 %collective-permute-start.49 = (bf16[4,320,384]{2,1,0:T(8,128)(2,1)S(1)}, bf16[4,320,384]{2,1,0:T(8,128)(2,1)S(1)}, u32[]{:S(2)}, u32[]{:S(2)}) collective-permute-start(bf16[4,320,384]{2,1,0:T(8,128)(2,1)S(1)} %hand_over.8), channel_id=1, source_target_pairs={{0,1},{1,0},{2,3},{3,2},{4,5},{5,4},{6,7},{7,6},{8,9},{9,8},{10,11... | collective-permute-start | bytes 2949128 | tf_op jit(solution)/shard_map/ppermute | solution.py:31
  260.0 4.1 %collective-permute-done.44.refs_3_.refs_20_ = bf16[80,640]{1,0:T(8,128)(2,1)S(1)} collective-permute-done((bf16[80,640]{1,0:T(8,128)(2,1)S(1)}, bf16[80,640]{1,0:T(8,128)(2,1)S(1)}, u32[]{:S(2)}, u32[]{:S(2)}) %collective-permute-start.44) | collective-permute-done | bytes 102432 | tf_op jit(solution)/shard_map/ppermute | solution.py:31
  266.5 3.3 %collective-permute-done.7.refs_1_ = bf16[160,640]{1,0:T(8,128)(2,1)S(1)} collective-permute-done((bf16[160,640]{1,0:T(8,128)(2,1)S(1)}, bf16[160,640]{1,0:T(8,128)(2,1)S(1)}, u32[]{:S(2)}, u32[]{:S(2)}) %collective-permute-start.7) | collective-permute-done | bytes 204832 | tf_op jit(solution)/shard_map/ppermute | solution.py:31
  269.8 3.1 %collective-permute-start.50 = (bf16[4,160,384]{2,1,0:T(8,128)(2,1)S(1)}, bf16[4,160,384]{2,1,0:T(8,128)(2,1)S(1)}, u32[]{:S(2)}, u32[]{:S(2)}) collective-permute-start(bf16[4,160,384]{2,1,0:T(8,128)(2,1)S(1)} %hand_over.9), channel_id=1, source_target_pairs={{0,1},{1,0},{2,3},{3,2},{4,5},{5,4},{6,7},{7,6},{8,9},{9,8},{10,11... | collective-permute-start | bytes 1474568 | tf_op jit(solution)/shard_map/ppermute | solution.py:31
  281.4 9.1 %mix.1 = f32[2,320,2560]{2,1,0:T(8,128)} custom-call(s32[13]{0:T(128)} %copy-done.31, f32[2,4]{1,0:T(2,128)} %w_ref.1, bf16[160,640]{1,0:T(8,128)(2,1)} %copy-done.15, bf16[160,640]{1,0:T(8,128)(2,1)} %copy-done.27, bf16[160,640]{1,0:T(8,128)(2,1)} %copy-done.26, bf16[160,640]{1,0:T(8,128)(2,1)} %copy-done.28, bf16[320,640]{1,0:T(8,128)(2,1)} %copy-done.3, ...), custom_call_target="tpu_custom_call" | custom-call | tf_op jit(solution)/shard_map/mix/pallas_call | solution.py:388
  (180 shorter events, 61.4 us)
Async XLA Ops:
  0.0 83.4 %collective-permute-start.3 = (bf16[512,4096]{1,0:T(8,128)(2,1)}, bf16[512,4096]{1,0:T(8,128)(2,1)}, u32[]{:S(2)}, u32[]{:S(2)}) collective-permute-start(bf16[512,4096]{1,0:T(8,128)(2,1)} %bitcast.40), channel_id=1, source_target_pairs={{0,1},{1,0},{2,3},{3,2},{4,5},{5,4},{6,7},{7,6},{8,9},{9,8},{10,11... | collective-permute-start | bytes 12582920 | tf_op jit(solution)/shard_map/ppermute | solution.py:31
  0.8 19.5 %collective-permute-start.1 = (bf16[80,4096]{1,0:T(8,128)(2,1)}, bf16[80,4096]{1,0:T(8,128)(2,1)}, u32[]{:S(2)}, u32[]{:S(2)}) collective-permute-start(bf16[80,4096]{1,0:T(8,128)(2,1)} %refs_1_.1), channel_id=1, source_target_pairs={{0,0},{1,1},{2,4},{3,5},{4,2},{5,3},{6,6},{7,7},{8,8},{9,9},{10,12... | collective-permute-start | bytes 1966088 | tf_op jit(solution)/shard_map/ppermute | solution.py:31
  18.5 37.3 %collective-permute-start.12 = (bf16[80,4096]{1,0:T(8,128)(2,1)}, bf16[80,4096]{1,0:T(8,128)(2,1)}, u32[]{:S(2)}, u32[]{:S(2)}) collective-permute-start(bf16[80,4096]{1,0:T(8,128)(2,1)} %refs_1_.1), channel_id=1, source_target_pairs={{0,8},{1,9},{2,10},{3,11},{4,12},{5,13},{6,14},{7,15},{8,0},{9,1},... | collective-permute-start | bytes 1966088 | tf_op jit(solution)/shard_map/ppermute | solution.py:31
  20.3 76.3 %collective-permute-start.4 = (bf16[2560,512]{1,0:T(8,128)(2,1)}, bf16[2560,512]{1,0:T(8,128)(2,1)S(1)}, u32[]{:S(2)}, u32[]{:S(2)}) collective-permute-start(bf16[2560,512]{1,0:T(8,128)(2,1)} %own_ref.9), channel_id=1, source_target_pairs={{0,1},{1,0},{2,3},{3,2},{4,5},{5,4},{6,7},{7,6},{8,9},{9,8},{10,11... | collective-permute-start | bytes 7864328 | tf_op jit(solution)/shard_map/ppermute | solution.py:31
  21.2 32.3 %collective-permute-start.10 = (bf16[80,4096]{1,0:T(8,128)(2,1)}, bf16[80,4096]{1,0:T(8,128)(2,1)S(1)}, u32[]{:S(2)}, u32[]{:S(2)}) collective-permute-start(bf16[80,4096]{1,0:T(8,128)(2,1)} %collective-permute-done.refs_1_.refs_0_), channel_id=1, source_target_pairs={{0,0},{1,1},{2,4},{3,5},{4,2},{5,3},{6,6},{7,7},{8,8},{9,9},{10,12... | collective-permute-start | bytes 1966088 | tf_op jit(solution)/shard_map/ppermute | solution.py:31
  55.9 26.3 %collective-permute-start.14 = (bf16[80,4096]{1,0:T(8,128)(2,1)S(1)}, bf16[80,4096]{1,0:T(8,128)(2,1)}, u32[]{:S(2)}, u32[]{:S(2)}) collective-permute-start(bf16[80,4096]{1,0:T(8,128)(2,1)S(1)} %broadcast_select_fusion.3.refs_2_), channel_id=1, source_target_pairs={{0,8},{1,9},{2,10},{3,11},{4,12},{5,13},{6,14},{7,15},{8,0},{9,1},... | collective-permute-start | bytes 1966088 | tf_op jit(solution)/shard_map/ppermute | solution.py:31
  67.8 43.4 %collective-permute-start.30 = (bf16[80,4096]{1,0:T(8,128)(2,1)}, bf16[80,4096]{1,0:T(8,128)(2,1)}, u32[]{:S(2)}, u32[]{:S(2)}) collective-permute-start(bf16[80,4096]{1,0:T(8,128)(2,1)} %get-tuple-element.26), channel_id=1, source_target_pairs={{0,8},{1,9},{2,10},{3,11},{4,12},{5,13},{6,14},{7,15},{8,0},{9,1},... | collective-permute-start | bytes 1966088 | tf_op jit(solution)/shard_map/ppermute | solution.py:31
  70.8 40.7 %collective-permute-start.23 = (bf16[80,4096]{1,0:T(8,128)(2,1)}, bf16[80,4096]{1,0:T(8,128)(2,1)}, u32[]{:S(2)}, u32[]{:S(2)}) collective-permute-start(bf16[80,4096]{1,0:T(8,128)(2,1)} %broadcast_select_fusion.2.refs_2_), channel_id=1, source_target_pairs={{0,8},{1,9},{2,10},{3,11},{4,12},{5,13},{6,14},{7,15},{8,0},{9,1},... | collective-permute-start | bytes 1966088 | tf_op jit(solution)/shard_map/ppermute | solution.py:31
  82.2 29.5 %collective-permute-start.29 = (bf16[80,4096]{1,0:T(8,128)(2,1)}, bf16[80,4096]{1,0:T(8,128)(2,1)}, u32[]{:S(2)}, u32[]{:S(2)}) collective-permute-start(bf16[80,4096]{1,0:T(8,128)(2,1)} %broadcast_select_fusion.2.refs_2_), channel_id=1, source_target_pairs={{0,16},{1,17},{2,18},{3,19},{4,20},{5,21},{6,22},{7,23},{8,24},{9,... | collective-permute-start | bytes 1966088 | tf_op jit(solution)/shard_map/ppermute | solution.py:31
  83.4 29.8 %collective-permute-start.31 = (bf16[80,4096]{1,0:T(8,128)(2,1)}, bf16[80,4096]{1,0:T(8,128)(2,1)}, u32[]{:S(2)}, u32[]{:S(2)}) collective-permute-start(bf16[80,4096]{1,0:T(8,128)(2,1)} %collective-permute-done.14.refs_5_), channel_id=1, source_target_pairs={{0,16},{1,17},{2,18},{3,19},{4,20},{5,21},{6,22},{7,23},{8,24},{9,... | collective-permute-start | bytes 1966088 | tf_op jit(solution)/shard_map/ppermute | solution.py:31
  96.6 28.4 %collective-permute-start.22 = (bf16[80,4096]{1,0:T(8,128)(2,1)S(1)}, bf16[80,4096]{1,0:T(8,128)(2,1)S(1)}, u32[]{:S(2)}, u32[]{:S(2)}) collective-permute-start(bf16[80,4096]{1,0:T(8,128)(2,1)S(1)} %copy-done.11), channel_id=1, source_target_pairs={{0,16},{1,17},{2,18},{3,19},{4,20},{5,21},{6,22},{7,23},{8,24},{9,... | collective-permute-start | bytes 1966088 | tf_op jit(solution)/shard_map/ppermute | solution.py:31
  111.2 27.1 %collective-permute-start.38 = (bf16[80,4096]{1,0:T(8,128)(2,1)S(1)}, bf16[80,4096]{1,0:T(8,128)(2,1)S(1)}, u32[]{:S(2)}, u32[]{:S(2)}) collective-permute-start(bf16[80,4096]{1,0:T(8,128)(2,1)S(1)} %copy-done.35), channel_id=1, source_target_pairs={{0,8},{1,9},{2,10},{3,11},{4,12},{5,13},{6,14},{7,15},{8,0},{9,1},... | collective-permute-start | bytes 1966088 | tf_op jit(solution)/shard_map/ppermute | solution.py:31
  111.5 26.9 %collective-permute-start.39 = (bf16[80,4096]{1,0:T(8,128)(2,1)}, bf16[80,4096]{1,0:T(8,128)(2,1)S(1)}, u32[]{:S(2)}, u32[]{:S(2)}) collective-permute-start(bf16[80,4096]{1,0:T(8,128)(2,1)} %collective-permute-done.23.refs_5_), channel_id=1, source_target_pairs={{0,16},{1,17},{2,18},{3,19},{4,20},{5,21},{6,22},{7,23},{8,24},{9,... | collective-permute-start | bytes 1966088 | tf_op jit(solution)/shard_map/ppermute | solution.py:31
  111.7 38.0 %collective-permute-start.5 = (bf16[2,160,640]{2,1,0:T(8,128)(2,1)S(1)}, bf16[2,160,640]{2,1,0:T(8,128)(2,1)S(1)}, u32[]{:S(2)}, u32[]{:S(2)}) collective-permute-start(bf16[2,160,640]{2,1,0:T(8,128)(2,1)S(1)} %get-tuple-element.16), channel_id=1, source_target_pairs={{0,2},{1,3},{2,0},{3,1},{4,6},{5,7},{6,4},{7,5},{8,10},{9,11},{10,... | collective-permute-start | bytes 1228808 | tf_op jit(solution)/shard_map/ppermute | solution.py:31
  113.2 36.6 %collective-permute-start.15 = (bf16[2,320,640]{2,1,0:T(8,128)(2,1)S(1)}, bf16[2,320,640]{2,1,0:T(8,128)(2,1)S(1)}, u32[]{:S(2)}, u32[]{:S(2)}) collective-permute-start(bf16[2,320,640]{2,1,0:T(8,128)(2,1)S(1)} %get-tuple-element.18), channel_id=1, source_target_pairs={{0,2},{1,3},{2,0},{3,1},{4,6},{5,7},{6,4},{7,5},{8,10},{9,11},{10,... | collective-permute-start | bytes 2457608 | tf_op jit(solution)/shard_map/ppermute | solution.py:31
  125.0 26.4 %collective-permute-start.32 = (bf16[2,320,640]{2,1,0:T(8,128)(2,1)S(1)}, bf16[2,320,640]{2,1,0:T(8,128)(2,1)S(1)}, u32[]{:S(2)}, u32[]{:S(2)}) collective-permute-start(bf16[2,320,640]{2,1,0:T(8,128)(2,1)S(1)} %get-tuple-element.22), channel_id=1, source_target_pairs={{0,2},{1,3},{2,0},{3,1},{4,6},{5,7},{6,4},{7,5},{8,10},{9,11},{10,... | collective-permute-start | bytes 2457608 | tf_op jit(solution)/shard_map/ppermute | solution.py:31
  138.3 30.7 %collective-permute-start.24 = (bf16[2,320,640]{2,1,0:T(8,128)(2,1)S(1)}, bf16[2,320,640]{2,1,0:T(8,128)(2,1)S(1)}, u32[]{:S(2)}, u32[]{:S(2)}) collective-permute-start(bf16[2,320,640]{2,1,0:T(8,128)(2,1)S(1)} %get-tuple-element.20), channel_id=1, source_target_pairs={{0,2},{1,3},{2,0},{3,1},{4,6},{5,7},{6,4},{7,5},{8,10},{9,11},{10,... | collective-permute-start | bytes 2457608 | tf_op jit(solution)/shard_map/ppermute | solution.py:31
  148.3 30.9 %collective-permute-start.40 = (bf16[2,160,640]{2,1,0:T(8,128)(2,1)S(1)}, bf16[2,160,640]{2,1,0:T(8,128)(2,1)S(1)}, u32[]{:S(2)}, u32[]{:S(2)}) collective-permute-start(bf16[2,160,640]{2,1,0:T(8,128)(2,1)S(1)} %get-tuple-element.24), channel_id=1, source_target_pairs={{0,2},{1,3},{2,0},{3,1},{4,6},{5,7},{6,4},{7,5},{8,10},{9,11},{10,... | collective-permute-start | bytes 1228808 | tf_op jit(solution)/shard_map/ppermute | solution.py:31
  149.9 20.5 %collective-permute-start.16 = (bf16[320,640]{1,0:T(8,128)(2,1)S(1)}, bf16[320,640]{1,0:T(8,128)(2,1)S(1)}, u32[]{:S(2)}, u32[]{:S(2)}) collective-permute-start(bf16[320,640]{1,0:T(8,128)(2,1)S(1)} %fusion.3), channel_id=1, source_target_pairs={{0,6},{1,7},{2,4},{3,5},{4,2},{5,3},{6,0},{7,1},{8,14},{9,15},{10,... | collective-permute-start | bytes 1228808 | tf_op jit(solution)/shard_map/ppermute | solution.py:31
  151.6 21.6 %collective-permute-start.33 = (bf16[320,640]{1,0:T(8,128)(2,1)S(1)}, bf16[320,640]{1,0:T(8,128)(2,1)S(1)}, u32[]{:S(2)}, u32[]{:S(2)}) collective-permute-start(bf16[320,640]{1,0:T(8,128)(2,1)S(1)} %fusion.5), channel_id=1, source_target_pairs={{0,6},{1,7},{2,4},{3,5},{4,2},{5,3},{6,0},{7,1},{8,14},{9,15},{10,... | collective-permute-start | bytes 1228808 | tf_op jit(solution)/shard_map/ppermute | solution.py:31
  170.6 48.9 %collective-permute-start.17 = (bf16[320,640]{1,0:T(8,128)(2,1)S(1)}, bf16[320,640]{1,0:T(8,128)(2,1)S(1)}, u32[]{:S(2)}, u32[]{:S(2)}) collective-permute-start(bf16[320,640]{1,0:T(8,128)(2,1)S(1)} %fusion.2.refs_0_.refs_4_), channel_id=1, source_target_pairs={{0,8},{1,9},{2,10},{3,11},{4,12},{5,13},{6,14},{7,15},{8,0},{9,1},... | collective-permute-start | bytes 1228808 | tf_op jit(solution)/shard_map/ppermute | solution.py:31
  171.9 48.9 %collective-permute-start.18 = (bf16[320,640]{1,0:T(8,128)(2,1)S(1)}, bf16[320,640]{1,0:T(8,128)(2,1)S(1)}, u32[]{:S(2)}, u32[]{:S(2)}) collective-permute-start(bf16[320,640]{1,0:T(8,128)(2,1)S(1)} %fusion.2.refs_0_.refs_4_), channel_id=1, source_target_pairs={{0,16},{1,17},{2,18},{3,19},{4,20},{5,21},{6,22},{7,23},{8,24},{9,... | collective-permute-start | bytes 1228808 | tf_op jit(solution)/shard_map/ppermute | solution.py:31
  179.1 41.9 %collective-permute-start.27 = (bf16[320,640]{1,0:T(8,128)(2,1)S(1)}, bf16[320,640]{1,0:T(8,128)(2,1)S(1)}, u32[]{:S(2)}, u32[]{:S(2)}) collective-permute-start(bf16[320,640]{1,0:T(8,128)(2,1)S(1)} %fusion.1.refs_0_.refs_8_), channel_id=1, source_target_pairs={{0,16},{1,17},{2,18},{3,19},{4,20},{5,21},{6,22},{7,23},{8,24},{9,... | collective-permute-start | bytes 1228808 | tf_op jit(solution)/shard_map/ppermute | solution.py:31
  184.8 33.6 %collective-permute-start.41 = (bf16[160,640]{1,0:T(8,128)(2,1)S(1)}, bf16[160,640]{1,0:T(8,128)(2,1)S(1)}, u32[]{:S(2)}, u32[]{:S(2)}) collective-permute-start(bf16[160,640]{1,0:T(8,128)(2,1)S(1)} %fusion.9), channel_id=1, source_target_pairs={{0,6},{1,7},{2,4},{3,5},{4,2},{5,3},{6,0},{7,1},{8,14},{9,15},{10,... | collective-permute-start | bytes 614408 | tf_op jit(solution)/shard_map/ppermute | solution.py:31
  192.1 46.5 %collective-permute-start.26 = (bf16[320,640]{1,0:T(8,128)(2,1)S(1)}, bf16[320,640]{1,0:T(8,128)(2,1)S(1)}, u32[]{:S(2)}, u32[]{:S(2)}) collective-permute-start(bf16[320,640]{1,0:T(8,128)(2,1)S(1)} %fusion.1.refs_0_.refs_8_), channel_id=1, source_target_pairs={{0,8},{1,9},{2,10},{3,11},{4,12},{5,13},{6,14},{7,15},{8,0},{9,1},... | collective-permute-start | bytes 1228808 | tf_op jit(solution)/shard_map/ppermute | solution.py:31
  221.1 36.6 %collective-permute-start.28 = (bf16[320,640]{1,0:T(8,128)(2,1)S(1)}, bf16[320,640]{1,0:T(8,128)(2,1)S(1)}, u32[]{:S(2)}, u32[]{:S(2)}) collective-permute-start(bf16[320,640]{1,0:T(8,128)(2,1)S(1)} %collective-permute-done.27.refs_2_.refs_10_), channel_id=1, source_target_pairs={{0,8},{1,9},{2,10},{3,11},{4,12},{5,13},{6,14},{7,15},{8,0},{9,1},... | collective-permute-start | bytes 1228808 | tf_op jit(solution)/shard_map/ppermute | solution.py:31
  223.3 36.2 %collective-permute-start.42 = (bf16[160,640]{1,0:T(8,128)(2,1)S(1)}, bf16[160,640]{1,0:T(8,128)(2,1)S(1)}, u32[]{:S(2)}, u32[]{:S(2)}) collective-permute-start(bf16[160,640]{1,0:T(8,128)(2,1)S(1)} %fusion.6.refs_0_.refs_17_), channel_id=1, source_target_pairs={{0,8},{1,9},{2,10},{3,11},{4,12},{5,13},{6,14},{7,15},{8,0},{9,1},... | collective-permute-start | bytes 614408 | tf_op jit(solution)/shard_map/ppermute | solution.py:31
  226.2 32.7 %collective-permute-start.43 = (bf16[160,640]{1,0:T(8,128)(2,1)S(1)}, bf16[160,640]{1,0:T(8,128)(2,1)S(1)}, u32[]{:S(2)}, u32[]{:S(2)}) collective-permute-start(bf16[160,640]{1,0:T(8,128)(2,1)S(1)} %fusion.6.refs_0_.refs_17_), channel_id=1, source_target_pairs={{0,16},{1,17},{2,18},{3,19},{4,20},{5,21},{6,22},{7,23},{8,24},{9,... | collective-permute-start | bytes 614408 | tf_op jit(solution)/shard_map/ppermute | solution.py:31
  235.0 24.6 %collective-permute-start.8 = (bf16[160,640]{1,0:T(8,128)(2,1)S(1)}, bf16[160,640]{1,0:T(8,128)(2,1)S(1)}, u32[]{:S(2)}, u32[]{:S(2)}) collective-permute-start(bf16[160,640]{1,0:T(8,128)(2,1)S(1)} %fusion.7.refs_0_), channel_id=1, source_target_pairs={{0,16},{1,17},{2,18},{3,19},{4,20},{5,21},{6,22},{7,23},{8,24},{9,... | collective-permute-start | bytes 614408 | tf_op jit(solution)/shard_map/ppermute | solution.py:31
  238.6 39.8 %collective-permute-start.49 = (bf16[4,320,384]{2,1,0:T(8,128)(2,1)S(1)}, bf16[4,320,384]{2,1,0:T(8,128)(2,1)S(1)}, u32[]{:S(2)}, u32[]{:S(2)}) collective-permute-start(bf16[4,320,384]{2,1,0:T(8,128)(2,1)S(1)} %hand_over.8), channel_id=1, source_target_pairs={{0,1},{1,0},{2,3},{3,2},{4,5},{5,4},{6,7},{7,6},{8,9},{9,8},{10,11... | collective-permute-start | bytes 2949128 | tf_op jit(solution)/shard_map/ppermute | solution.py:31
  257.6 20.8 %collective-permute-start.47 = (bf16[4,320,384]{2,1,0:T(8,128)(2,1)S(1)}, bf16[4,320,384]{2,1,0:T(8,128)(2,1)S(1)}, u32[]{:S(2)}, u32[]{:S(2)}) collective-permute-start(bf16[4,320,384]{2,1,0:T(8,128)(2,1)S(1)} %hand_over.6), channel_id=1, source_target_pairs={{0,1},{1,0},{2,3},{3,2},{4,5},{5,4},{6,7},{7,6},{8,9},{9,8},{10,11... | collective-permute-start | bytes 2949128 | tf_op jit(solution)/shard_map/ppermute | solution.py:31
  259.0 21.4 %collective-permute-start.48 = (bf16[4,320,384]{2,1,0:T(8,128)(2,1)S(1)}, bf16[4,320,384]{2,1,0:T(8,128)(2,1)S(1)}, u32[]{:S(2)}, u32[]{:S(2)}) collective-permute-start(bf16[4,320,384]{2,1,0:T(8,128)(2,1)S(1)} %hand_over.7), channel_id=1, source_target_pairs={{0,1},{1,0},{2,3},{3,2},{4,5},{5,4},{6,7},{7,6},{8,9},{9,8},{10,11... | collective-permute-start | bytes 2949128 | tf_op jit(solution)/shard_map/ppermute | solution.py:31
  (57 other events, 1272.4 us)
